TPU v7x, 32 devices: a whole 2x2x4 slice. The times are simulated.
32 devices in a mesh: grp: 2 (over y), dp: 16 (over z, x, core).
Axes of the slice: x: 2, y: 2, z: 4, core: 2. Of those that a mesh axis runs over, the one named last changes fastest.
Arguments:
- teacher_states: bfloat16 [2, 4096, 6144], P(None, 'dp', 'grp'), may hold values from -18.5 to 18.5
- student_features: bfloat16 [2, 4096, 1024], P(None, 'dp'), may hold values from -13 to 13
- w_first: bfloat16 [1024, 1024], replicated, may hold values from -0.1875 to 0.1875
- w_second: bfloat16 [1024, 1024], replicated, may hold values from -0.1875 to 0.1875
Outputs:
- correlation: float32 [1024, 6144], P('dp', 'grp')
All inputs are finite; a program needn't handle non-finite values.
Results may differ from a plain program's by a relative error of at most 0.0003.
Values may be sent and summed in bfloat16 or wider, within the bound.
No kernel may reach another device: no remote copies, remote signals or barrier semaphores. Data moves between devices by JAX's collectives and lax.ppermute only.
A program may use at most 128 MiB of HBM per device.

v0:
```python
import math

import jax
import jax.numpy as jnp
from jax import lax
from jax.sharding import PartitionSpec as P

DT = 6144


EPSILON = 1e-06


def normalize_rows(states):
    values = states.astype(jnp.float32)
    sums = (jnp.sum(values, axis=1), jnp.sum(values * values, axis=1))
    totals = lax.psum((sums[0], sums[1]), "grp")
    row_mean = totals[0] / DT
    row_var = totals[1] / DT - row_mean * row_mean
    return (values - row_mean[:, None]) * lax.rsqrt(row_var + EPSILON)[:, None]


def teacher_side(states, token_total):
    normed = normalize_rows(states)
    power = lax.psum(jnp.sum(normed * normed, axis=0), "dp")
    return (normed * lax.rsqrt(power / token_total + EPSILON)).astype(jnp.bfloat16)


def project(features, w_first, w_second):
    hidden = jax.nn.gelu(jnp.dot(features, w_first, preferred_element_type=jnp.float32)).astype(
        jnp.bfloat16
    )
    return jnp.dot(hidden, w_second, preferred_element_type=jnp.float32)


def column_sums(projected):
    sums = (jnp.sum(projected, axis=0), jnp.sum(projected * projected, axis=0))
    return lax.psum((sums[0], sums[1]), "dp")


def standardize(projected, totals, token_total):
    col_mean = totals[0] / token_total
    col_var = totals[1] / token_total - col_mean * col_mean
    return ((projected - col_mean) * lax.rsqrt(col_var + EPSILON)).astype(jnp.bfloat16)


def student_side(features, w_first, w_second, token_total):
    projected = project(features, w_first, w_second)
    return standardize(projected, column_sums(projected), token_total)


def make_product(pair_list):
    running = None
    for student_z, teacher_z in pair_list:
        product = lax.dot_general(
            student_z, teacher_z, (((0,), (0,)), ((), ())), preferred_element_type=jnp.float32
        )
        running = product
    return running


def shards(teacher_states, student_features, w_first, w_second):
    micro_count = teacher_states.shape[0]
    token_total = teacher_states.shape[1] * lax.axis_size("dp")
    correlation = None
    for batch_index in range(micro_count):
        teacher_z = teacher_side(teacher_states[batch_index], token_total)
        student_z = student_side(student_features[batch_index], w_first, w_second, token_total)
        portion_sum = lax.psum_scatter(
            make_product([(student_z, teacher_z)]), "dp", scatter_dimension=0, tiled=True
        )
        correlation = portion_sum if correlation is None else correlation + portion_sum
    return correlation * (1.0 / math.sqrt(micro_count * token_total))


def solution(mesh):
    placed = (P(None, "dp", "grp"), P(None, "dp", None), P(), P())
    return jax.shard_map(
        shards, mesh=mesh, in_specs=placed, out_specs=P("dp", "grp"), check_vma=False
    )
```

profile of v0, /device:TPU:0, one launch (start us, length us, event | category | flops | bytes accessed | tf_op | source)
XLA Modules:
  0.0 245.8 jit_solution(2058709502384886520)
XLA Ops:
  6.5 0.0 copy-start
  6.5 0.0 reduce-scatter.2.cloned.1.call-start
  6.5 1.9 fusion.15
  8.5 2.4 convert_reduce_fusion
  10.9 0.0 copy-done
  10.9 3.3 %fusion.83 = (f32[1024]{0:T(1024)S(1)}, f32[1024]{0:T(1024)S(1)}, f32[256,1024]{1,0:T(8,128)S(1)}) fusion(bf16[1024,1024]{1,0:T(8,128)(2,1)S(1)} %copy-done, bf16[1024,1024]{1,0:T(8,128)(2,1)} %param.6, bf16[2,256,1024]{2,1,0:T(8,128)(2,1)} %param.5), kind=kOutput, calls=%fused_computation.91 | convolution fusion | flops 1076885504 | bytes 5775360 | tf_op jit(solution)/shard_map/dot_general | solution.py:33
  14.1 4.2 %fusion.84 = (f32[1024]{0:T(1024)S(1)}, f32[1024]{0:T(1024)S(1)}, f32[256,1024]{1,0:T(8,128)}) fusion(bf16[1024,1024]{1,0:T(8,128)(2,1)S(1)} %copy-done, bf16[1024,1024]{1,0:T(8,128)(2,1)} %param.6, bf16[2,256,1024]{2,1,0:T(8,128)(2,1)} %param.5), kind=kOutput, calls=%fused_computation.92 | convolution fusion | flops 1076885504 | bytes 5775360 | tf_op jit(solution)/shard_map/dot_general | solution.py:33
  18.4 5.9 %all-reduce.2 = (f32[256]{0:T(256)S(1)}, f32[256]{0:T(256)S(1)}) all-reduce(f32[256]{0:T(256)S(1)} %fusion.15, f32[256]{0:T(256)S(1)} %get-tuple-element.7), channel_id=1, replica_groups=mesh['grp'=2,'dp'=16] {'grp'}, use_global_device_ids=true, to_apply=%region_18.0 | all-reduce | flops 512 | bytes 4096 | tf_op jit(solution)/shard_map/psum | solution.py:17
  24.2 2.8 %fusion.13 = (f32[3072]{0:T(1024)S(1)}, f32[256]{0:T(256)S(1)}) fusion(f32[256]{0:T(256)S(1)} %get-tuple-element.30, f32[256]{0:T(256)S(1)} %get-tuple-element.29, bf16[2,256,3072]{2,1,0:T(8,128)(2,1)} %param.4), kind=kLoop, calls=%fused_computation.18 | loop fusion | flops 6288128 | bytes 3161088 | tf_op jit(solution)/shard_map/reduce_sum | solution.py:25
  27.1 4.9 %all-reduce.1 = (f32[256]{0:T(256)S(1)}, f32[256]{0:T(256)S(1)}) all-reduce(f32[256]{0:T(256)S(1)} %get-tuple-element.6, f32[256]{0:T(256)S(1)} %get-tuple-element.8), channel_id=1, replica_groups=mesh['grp'=2,'dp'=16] {'grp'}, use_global_device_ids=true, to_apply=%region_7.0 | all-reduce | flops 512 | bytes 4096 | tf_op jit(solution)/shard_map/psum | solution.py:17
  32.0 2.1 fusion.7
  34.1 59.7 %all-reduce = (f32[3072]{0:T(1024)S(1)}, f32[1024]{0:T(1024)S(1)}, f32[1024]{0:T(1024)S(1)}, f32[3072]{0:T(1024)S(1)}, f32[1024]{0:T(1024)S(1)}, /*index=5*/f32[1024]{0:T(1024)S(1)}) all-reduce(f32[3072]{0:T(1024)S(1)} %fusion.7, f32[1024]{0:T(1024)S(1)} %get-tuple-element.12, ...), channel_id=1, replica_groups=mesh['grp'=2,'dp'=16] {'dp'}, use_global_device_ids=true, to_apply=%region_9.0 | all-reduce | flops 10240 | bytes 81920 | tf_op jit(solution)/shard_map/psum | solution.py:25
  93.8 0.0 copy-start.1
  93.8 3.9 %fusion.17 = f32[1024,3072]{1,0:T(8,128)S(1)} fusion(f32[3072]{0:T(1024)S(1)} %get-tuple-element.34, f32[256]{0:T(256)S(1)} %get-tuple-element.28, f32[256]{0:T(256)S(1)} %get-tuple-element.27, bf16[2,256,3072]{2,1,0:T(8,128)(2,1)} %param.4, f32[256,1024]{1,0:T(8,128)} %get-tuple-element.31, f32[1024]{0:T(1024)S(1)} %get-tuple-element.35, ...), kind=kOutput, calls=%fused_computation.21 | convolution fusion | flops 1615331328 | bytes 15226880 | tf_op jit(solution)/shard_map/dot_general | solution.py:55
  97.7 0.0 copy-done.1
  97.8 6.7 %convolution_add_fusion = f32[1024,3072]{1,0:T(8,128)} fusion(f32[1024,3072]{1,0:T(8,128)S(1)} %fusion.17, f32[3072]{0:T(1024)S(1)} %get-tuple-element.33, f32[256]{0:T(256)S(1)} %get-tuple-element.30, f32[256]{0:T(256)S(1)} %get-tuple-element.29, bf16[2,256,3072]{2,1,0:T(8,128)(2,1)S(1)} %copy-done.1, f32[256,1024]{1,0:T(8,128)S(1)} %get-tuple-element.32, ...), kind=kOutput, calls=%fused_computation | convolution fusion | flops 1618477056 | bytes 27809792 | tf_op jit(solution)/shard_map/dot_general | solution.py:55
  104.5 0.0 reduce-scatter.2.cloned.1.call-update
  104.5 132.4 %reduce-scatter.2.cloned.1.call-done = f32[64,3072]{1,0:T(8,128)} async-done(((f32[1024,3072]{1,0:T(8,128)}), f32[64,3072]{1,0:T(8,128)}) %reduce-scatter.2.cloned.1.call-update) | async-done | bytes 786448 | tf_op jit(solution)/shard_map/reduce_scatter | solution.py:69
  236.9 2.1 broadcast_multiply_fusion
  (4 shorter events, 0.0 us)
Async XLA Ops:
  6.5 4.3 %copy-start = (bf16[1024,1024]{1,0:T(8,128)(2,1)S(1)}, bf16[1024,1024]{1,0:T(8,128)(2,1)}, u32[]{:S(2)}) copy-start(bf16[1024,1024]{1,0:T(8,128)(2,1)} %param.7) | copy-start | bytes 6291460
  6.5 230.4 %reduce-scatter.2.cloned.1.call-start = ((), (), s32[]{:S(2)}) async-start(), calls=%async_computation.1 | async-start | bytes 13369344 | tf_op jit(solution)/shard_map/reduce_scatter | solution.py:69
  93.8 3.9 %copy-start.1 = (bf16[2,256,3072]{2,1,0:T(8,128)(2,1)S(1)}, bf16[2,256,3072]{2,1,0:T(8,128)(2,1)}, u32[]{:S(2)}) copy-start(bf16[2,256,3072]{2,1,0:T(8,128)(2,1)} %param.4) | copy-start | bytes 9437188
Sparse Core Ops, SparseCore 0:
  104.6 132.2 reduce-scatter.1
where the time goes:
time: 246 us
  waiting for transfers between devices  132 us (54%)
  blocking collectives  70.5 us (29%)
  matrix products  18.1 us (7%)
  between operations  13.4 us (5%)
  other arithmetic  11.4 us (5%)
    reduce_scatter x1, waiting for transfers between devices, shards(): lax.psum_scatter(make_product([(student_z, teacher_z)]), 'dp', scatter_di...  132 us
    psum x1, blocking collectives, teacher_side(): power = lax.psum(jnp.sum(normed * normed, axis=0), 'dp')  59.7 us
    psum x2, blocking collectives, normalize_rows(): totals = lax.psum((sums[0], sums[1]), 'grp')  10.8 us
    dot_general x2, matrix products, make_product(): lax.dot_general(student_z, teacher_z, (((0,), (0,)), ((), ())), preferred...  10.6 us
    dot_general x2, matrix products, project(): return jnp.dot(hidden, w_second, preferred_element_type=jnp.float32)  7.49 us
    reduce_sum x2, other arithmetic, teacher_side(): power = lax.psum(jnp.sum(normed * normed, axis=0), 'dp')  4.93 us
  transfers between devices with their start and end apart: 1, of which 1 were waited for; matrix products, arithmetic and copies ran while one was open for 0% of the time, Pallas kernels for 0%

commit v1 on v0

v1 whole, which is shorter than its diff:
```python
import math

import jax
import jax.numpy as jnp
from jax import lax
from jax.sharding import PartitionSpec as P

EPSILON = 1e-06
LIFT = 256.0
CHUNKS = ((0.25, False), (0.25, True), (0.25, False), (0.25, False))


def swap(value, axis, bit):
    size = lax.axis_size(axis)
    return lax.ppermute(value, axis, [(d, d ^ bit) for d in range(size)])


def shards(teacher, features, w_first, w_second):
    mb, tok, width = teacher.shape
    ds = w_second.shape[1]
    n = lax.axis_size("dp")
    grp = lax.axis_size("grp")
    me = lax.axis_index("dp")
    levels = n.bit_length() - 1
    hops = levels - 1
    rows = ds // n
    token_total = tok * n
    blocks = n // 2

    partner_x = swap(teacher, "dp", 1)

    x = teacher.astype(jnp.float32)
    sums = jnp.stack([jnp.sum(x, axis=2), jnp.sum(x * x, axis=2)])
    sums = sums + swap(sums, "grp", 1)
    mean = sums[0] / (width * grp)
    rstd = lax.rsqrt(sums[1] / (width * grp) - mean * mean + EPSILON)

    hidden = jax.nn.gelu(
        jnp.dot(features.reshape(mb * tok, -1), w_first, preferred_element_type=jnp.float32)
    ).astype(jnp.bfloat16)
    partner_hidden = swap(hidden, "dp", 1)

    index = jnp.arange(blocks)
    distance = jnp.zeros_like(index)
    for h in range(hops):
        distance = distance + (((index >> (hops - 1 - h)) & 1) << (h + 1))
    owner = me ^ distance
    source = (owner[:, None] * rows + jnp.arange(rows)[None, :]).reshape(-1)
    select = (source[:, None] == jnp.arange(ds)[None, :]).astype(jnp.bfloat16)
    w_sel = lax.dot_general(
        select, w_second, (((1,), (1,)), ((), ())), preferred_element_type=jnp.float32
    ).astype(jnp.bfloat16)
    project = lambda h: lax.dot_general(
        w_sel, h, (((1,), (1,)), ((), ())), preferred_element_type=jnp.float32
    ).reshape(blocks * rows, mb, tok)
    proj = project(hidden), project(partner_hidden)
    s1 = sum(jnp.sum(p, axis=2) for p in proj)
    s2 = sum(jnp.sum(p * p, axis=2) for p in proj)
    student = jnp.stack([s1, s2])

    normed = (x - mean[..., None]) * rstd[..., None]
    power = jnp.sum(normed * normed, axis=1)
    first = jnp.concatenate([power.reshape(-1), mean.reshape(-1), rstd.reshape(-1)])
    got = swap(first, "dp", 1)
    count = mb * width
    power = power.reshape(-1) + got[:count]
    p_mean = got[count : count + mb * tok].reshape(mb, tok)
    p_rstd = got[count + mb * tok :].reshape(mb, tok)

    bits = (2,) * hops
    for h in range(hops):
        got = swap(jnp.concatenate([power, student.reshape(-1)]), "dp", 2 << h)
        power = power + got[:count]
        theirs = got[count:].reshape((2,) + bits + (rows, mb))
        student = (student.reshape((2,) + bits + (rows, mb)) + jnp.flip(theirs, axis=1 + h))
    student = student.reshape(2, blocks * rows, mb)
    col_mean = student[0] / token_total
    col_scale = lax.rsqrt(student[1] / token_total - col_mean * col_mean + EPSILON)
    z = [
        ((p - col_mean[..., None]) * col_scale[..., None])
        .astype(jnp.bfloat16)
        .reshape(blocks * rows, mb * tok)
        for p in proj
    ]
    scale = lax.rsqrt(power.reshape(mb, 1, width) / token_total + EPSILON)
    factor = LIFT / math.sqrt(mb * token_total)

    pieces = []
    start = 0
    for share, late in CHUNKS:
        size = int(width * share)
        cols = slice(start, start + size)
        start += size
        product = None
        for zi, xi, mi, ri in (
            (z[0], teacher, mean, rstd),
            (z[1], partner_x, p_mean, p_rstd),
        ):
            tz = (
                (xi[:, :, cols].astype(jnp.float32) - mi[..., None]) * ri[..., None] * scale[:, :, cols]
            ).astype(jnp.bfloat16)
            part = jnp.dot(zi, tz.reshape(mb * tok, size), preferred_element_type=jnp.float32)
            product = part if product is None else product + part
        product = (product * factor).reshape(bits + (rows, size))
        order = list(range(1, hops)) + [0] if late else list(range(hops))
        held = product
        for h in order:
            keep = lax.index_in_dim(held, 0, h, keepdims=True)
            send = lax.index_in_dim(held, 1, h, keepdims=True).astype(jnp.float16)
            held = keep + swap(send, "dp", 2 << h).astype(jnp.float32)
        pieces.append(held.reshape(rows, size) * (1.0 / LIFT))
    return jnp.concatenate(pieces, axis=1)


def solution(mesh):
    placed = (P(None, "dp", "grp"), P(None, "dp", None), P(), P())
    return jax.shard_map(
        shards, mesh=mesh, in_specs=placed, out_specs=P("dp", "grp"), check_vma=False
    )
```

time: 246 us -> 95.9 us (0.39)
  waiting for transfers between devices: 132 us -> 19.6 us
  blocking collectives: 70.5 us -> 0 us
  starting transfers between devices: 0.01 us -> 30.6 us
  between operations: 13.4 us -> 0.47 us
  local copies, waits for them, and re-layouts: 0.01 us -> 10.8 us
  matrix products: 18.1 us -> 22.7 us
    reduce_scatter x1 -> x0, waiting for transfers between devices: 132 us -> none  [shards(): lax.psum_scatter(make_product([(student_z, teacher_z)]), 'dp', scatter_di...]
    psum x3 -> x0, blocking collectives: 70.5 us -> none  [the longest x1 59.7 us: teacher_side(): power = lax.psum(jnp.sum(normed * normed, axis=0), 'dp')]
    ppermute x0 -> x19, starting transfers between devices: none -> 30.6 us  [swap(): return lax.ppermute(value, axis, [(d, d ^ bit) for d in range(size)])]
    ppermute x0 -> x19, waiting for transfers between devices: none -> 19.6 us  [swap(): return lax.ppermute(value, axis, [(d, d ^ bit) for d in range(size)])]
    reduce_sum x4 -> x2, other arithmetic: 9.24 us -> 2.54 us  [the longest x1 1.53 us: shards(): power = jnp.sum(normed * normed, axis=1)]
    dot_general x4 -> x12, matrix products: 18.1 us -> 22.7 us  [the longest x8 10.9 us: shards(): jnp.dot(zi, tz.reshape(mb * tok, size), preferred_element_type=jnp.float32)]
    reshape x0 -> x6, local copies, waits for them, and re-layouts: none -> 4.04 us  [the longest x3 2.2 us: shards(): theirs = got[count:].reshape((2,) + bits + (rows, mb))]
    unnamed x4 -> x21, local copies, waits for them, and re-layouts: 0.01 us -> 3.35 us
  transfers between devices with their start and end apart: 1 -> 19, of which waited for: 1 -> 9; matrix products, arithmetic and copies ran while one was open for 0% -> 30% of each run, Pallas kernels for 0% -> 0%
where the time goes in v1:
time: 95.9 us; the launch traced here: 94.3 us
  starting transfers between devices  30.6 us (32%)
  matrix products  22.7 us (24%)
  waiting for transfers between devices  19.6 us (20%)
  local copies, waits for them, and re-layouts  10.8 us (11%)
  other arithmetic  10.2 us (11%)
    ppermute x19, starting transfers between devices, swap(): return lax.ppermute(value, axis, [(d, d ^ bit) for d in range(size)])  30.6 us
    ppermute x19, waiting for transfers between devices, swap(): return lax.ppermute(value, axis, [(d, d ^ bit) for d in range(size)])  19.6 us
    dot_general x8, matrix products, shards(): jnp.dot(zi, tz.reshape(mb * tok, size), preferred_element_type=jnp.float32)  10.9 us
    dot_general x2, matrix products, shards(): lax.dot_general(w_sel, h, (((1,), (1,)), ((), ())), preferred_element_typ...  4.72 us
    dot_general x1, matrix products, shards(): jnp.dot(features.reshape(mb * tok, -1), w_first, preferred_element_type=j...  4 us
    unnamed x21, local copies, waits for them, and re-layouts  3.35 us
    dot_general x1, matrix products, shards(): lax.dot_general(select, w_second, (((1,), (1,)), ((), ())), preferred_ele...  3.03 us
    reshape x3, local copies, waits for them, and re-layouts, shards(): theirs = got[count:].reshape((2,) + bits + (rows, mb))  2.2 us
  transfers between devices with their start and end apart: 19, of which 9 were waited for; matrix products, arithmetic and copies ran while one was open for 30% of the time, Pallas kernels for 0%

profile of v1, /device:TPU:0, one launch (start us, length us, event | category | flops | bytes accessed | tf_op | source)
XLA Modules:
  0.0 94.3 jit_solution(11237203141426048598)
XLA Ops:
  0.0 1.6 %copy-done = bf16[1024,1024]{1,0:T(8,128)(2,1)S(1)} copy-done((bf16[1024,1024]{1,0:T(8,128)(2,1)S(1)}, bf16[1024,1024]{1,0:T(8,128)(2,1)}, u32[]{:S(2)}) %copy-start) | copy-done | bytes 2097176
  1.6 4.0 %fusion.11 = bf16[512,1024]{1,0:T(8,128)(2,1)} fusion(bf16[512,1024]{1,0:T(8,128)(2,1)} %bitcast.151, bf16[1024,1024]{1,0:T(8,128)(2,1)S(1)} %copy-done), kind=kOutput, calls=%fused_computation.15 | convolution fusion | flops 1078460416 | bytes 4194304 | tf_op jit(solution)/shard_map/dot_general | solution.py:39
  7.1 2.6 %collective-permute-start.1 = (f32[2,2,256]{2,1,0:T(2,128)S(1)}, f32[2,2,256]{2,1,0:T(2,128)S(1)}, u32[]{:S(2)}, u32[]{:S(2)}) collective-permute-start(f32[2,2,256]{2,1,0:T(2,128)S(1)} %pad_maximum_fusion.6), channel_id=1, source_target_pairs={{0,16},{16,0},{1,17},{17,1},{2,18},{18,2},{3,19},{19,3},{4,20},{20... | collective-permute-start | bytes 12296 | tf_op jit(solution)/shard_map/ppermute | solution.py:15
  9.8 3.0 %fusion.17 = bf16[512,1024]{1,0:T(8,128)(2,1)S(1)} fusion(bf16[1024,1024]{1,0:T(8,128)(2,1)} %param.7, s32[512]{0:T(512)S(1)} %add.243), kind=kOutput, calls=%fused_computation.34 | convolution fusion | flops 1074790400 | bytes 3147776 | tf_op jit(solution)/shard_map/dot_general | solution.py:50
  13.0 1.5 %fusion.3 = f32[2,3072]{1,0:T(2,128)S(1)} fusion(bf16[2,256,3072]{2,1,0:T(8,128)(2,1)S(1)} %copy-done.2, f32[2,256]{1,0:T(2,128)S(1)} %fusion.74, f32[2,256]{1,0:T(2,128)S(1)} %get-tuple-element.35), kind=kLoop, calls=%fused_computation.6 | loop fusion | flops 7858176 | bytes 3174400 | tf_op jit(solution)/shard_map/reduce_sum | solution.py:62
  14.8 2.9 %bitcast_reduce_fusion.1 = (f32[512,2]{0,1:T(2,128)S(1)}, f32[512,2]{0,1:T(2,128)S(1)}, f32[512,512]{0,1:T(8,128)}) fusion(bf16[512,1024]{1,0:T(8,128)(2,1)S(1)} %fusion.17, bf16[512,1024]{1,0:T(8,128)(2,1)} %fusion.11), kind=kOutput, calls=%fused_computation.43 | convolution fusion | flops 537655296 | bytes 3153920 | tf_op jit(solution)/shard_map/dot_general | solution.py:53
  17.8 1.8 %bitcast_reduce_fusion = (f32[512,2]{0,1:T(2,128)S(1)}, f32[512,2]{0,1:T(2,128)S(1)}, f32[512,512]{0,1:T(8,128)}) fusion(bf16[512,1024]{1,0:T(8,128)(2,1)S(1)} %fusion.17, bf16[512,1024]{1,0:T(8,128)(2,1)S(1)} %collective-permute-done), kind=kOutput, calls=%fused_computation.37 | convolution fusion | flops 537655296 | bytes 3153920 | tf_op jit(solution)/shard_map/dot_general | solution.py:53
  20.1 1.6 %collective-permute-start.3 = (f32[8192]{0:T(1024)S(1)}, f32[8192]{0:T(1024)S(1)}, u32[]{:S(2)}, u32[]{:S(2)}) collective-permute-start(f32[8192]{0:T(1024)S(1)} %pad_maximum_fusion.1), channel_id=1, source_target_pairs={{0,2},{1,3},{2,0},{3,1},{4,6},{5,7},{6,4},{7,5},{8,10},{9,11},{10,... | collective-permute-start | bytes 98312 | tf_op jit(solution)/shard_map/ppermute | solution.py:15
  22.0 2.1 %collective-permute-done.3 = f32[8192]{0:T(1024)S(1)} collective-permute-done((f32[8192]{0:T(1024)S(1)}, f32[8192]{0:T(1024)S(1)}, u32[]{:S(2)}, u32[]{:S(2)}) %collective-permute-start.3) | collective-permute-done | bytes 32800 | tf_op jit(solution)/shard_map/ppermute | solution.py:15
  25.5 1.3 %reshape.366 = f32[2048]{0:T(1024)S(1)} reshape(f32[2,2,2,2,64,2]{5,4,3,2,1,0:T(8,128)} %maximum_add_fusion) | data formatting | bytes 16384 | tf_op jit(solution)/shard_map/reshape | solution.py:72
  26.8 1.6 %collective-permute-start.4 = (f32[8192]{0:T(1024)S(1)}, f32[8192]{0:T(1024)S(1)}, u32[]{:S(2)}, u32[]{:S(2)}) collective-permute-start(f32[8192]{0:T(1024)S(1)} %pad_maximum_fusion.2), channel_id=1, source_target_pairs={{0,4},{1,5},{2,6},{3,7},{4,0},{5,1},{6,2},{7,3},{8,12},{9,13},{10,... | collective-permute-start | bytes 98312 | tf_op jit(solution)/shard_map/ppermute | solution.py:15
  28.4 2.3 %collective-permute-done.4 = f32[8192]{0:T(1024)S(1)} collective-permute-done((f32[8192]{0:T(1024)S(1)}, f32[8192]{0:T(1024)S(1)}, u32[]{:S(2)}, u32[]{:S(2)}) %collective-permute-start.4) | collective-permute-done | bytes 32800 | tf_op jit(solution)/shard_map/ppermute | solution.py:15
  31.4 1.3 %reshape.367 = f32[2,2,2,2,64,2]{5,4,3,2,1,0:T(8,128)} reshape(f32[2048]{0:T(1024)S(1)} %slice.292) | data formatting | bytes 16384 | tf_op jit(solution)/shard_map/reshape | solution.py:74
  34.9 2.6 %collective-permute-start.5 = (f32[8192]{0:T(1024)S(1)}, f32[8192]{0:T(1024)S(1)}, u32[]{:S(2)}, u32[]{:S(2)}) collective-permute-start(f32[8192]{0:T(1024)S(1)} %pad_maximum_fusion.3), channel_id=1, source_target_pairs={{0,8},{1,9},{2,10},{3,11},{4,12},{5,13},{6,14},{7,15},{8,0},{9,1},... | collective-permute-start | bytes 98312 | tf_op jit(solution)/shard_map/ppermute | solution.py:15
  38.3 1.4 %collective-permute-done.5 = f32[8192]{0:T(1024)S(1)} collective-permute-done((f32[8192]{0:T(1024)S(1)}, f32[8192]{0:T(1024)S(1)}, u32[]{:S(2)}, u32[]{:S(2)}) %collective-permute-start.5) | collective-permute-done | bytes 32800 | tf_op jit(solution)/shard_map/ppermute | solution.py:15
  43.7 1.7 %fusion.20 = (bf16[512,2,256]{0,2,1:T(8,128)(2,1)S(1)}, bf16[512,2,256]{0,2,1:T(8,128)(2,1)S(1)}) fusion(f32[512,512]{0,1:T(8,128)} %get-tuple-element.37, f32[512,2]{0,1:T(2,128)S(1)} %add_rsqrt_fusion.1, f32[512,2]{0,1:T(2,128)S(1)} %copy.61, f32[512,512]{0,1:T(8,128)S(1)} %copy-done.5), kind=kLoop, calls=%fused_computation.40 | loop fusion | flops 1572864 | bytes 3153920 | tf_op jit(solution)/shard_map/convert_element_type | solution.py:81
  49.2 1.9 %fusion.13 = f32[512,768]{1,0:T(8,128)S(1)} fusion(f32[512,768,1]{1,0,2:T(8,128)S(1)} %fusion.28, bf16[512,2,256]{0,2,1:T(8,128)(2,1)S(1)} %get-tuple-element.31, bf16[2,256,3072]{2,1,0:T(8,128)(2,1)} %collective-permute-done.6, f32[2,768]{1,0:T(2,128)S(1)} %get-tuple-element.28, f32[2,256]{1,0:T(2,128)S(1)} %slice.250, f32[2,256]{1,0:T(2,128)S(1)} %slice.248), kind=kOutput, calls=%fused_computation.19 | convolution fusion | flops 405405696 | bytes 4466688 | tf_op jit(solution)/shard_map/dot_general | solution.py:102
  51.2 1.6 %collective-permute-start.16 = (f16[1,2,2,64,768]{4,3,2,1,0:T(8,128)(2,1)S(1)}, f16[1,2,2,64,768]{4,3,2,1,0:T(8,128)(2,1)S(1)}, u32[]{:S(2)}, u32[]{:S(2)}) collective-permute-start(f16[1,2,2,64,768]{4,3,2,1,0:T(8,128)(2,1)S(1)} %bitcast.138), channel_id=1, source_target_pairs={{0,2},{1,3},{2,0},{3,1},{4,6},{5,7},{6,4},{7,5},{8,10},{9,11},{10,... | collective-permute-start | bytes 1179656 | tf_op jit(solution)/shard_map/ppermute | solution.py:15
  52.7 1.9 %fusion.14 = f32[512,768]{1,0:T(8,128)S(1)} fusion(f32[512,768,1]{1,0,2:T(8,128)S(1)} %fusion.27, bf16[512,2,256]{0,2,1:T(8,128)(2,1)S(1)} %get-tuple-element.31, bf16[2,256,3072]{2,1,0:T(8,128)(2,1)} %collective-permute-done.6, f32[2,768]{1,0:T(2,128)S(1)} %get-tuple-element.29, f32[2,256]{1,0:T(2,128)S(1)} %slice.250, f32[2,256]{1,0:T(2,128)S(1)} %slice.248), kind=kOutput, calls=%fused_computation.21 | convolution fusion | flops 405405696 | bytes 4466688 | tf_op jit(solution)/shard_map/dot_general | solution.py:102
  55.4 1.9 %fusion.15 = f32[512,768]{1,0:T(8,128)S(1)} fusion(f32[512,768,1]{1,0,2:T(8,128)S(1)} %fusion.26, bf16[512,2,256]{0,2,1:T(8,128)(2,1)S(1)} %get-tuple-element.31, bf16[2,256,3072]{2,1,0:T(8,128)(2,1)} %collective-permute-done.6, f32[2,768]{1,0:T(2,128)S(1)} %get-tuple-element.30, f32[2,256]{1,0:T(2,128)S(1)} %slice.250, f32[2,256]{1,0:T(2,128)S(1)} %slice.248), kind=kOutput, calls=%fused_computation.23 | convolution fusion | flops 405405696 | bytes 4466688 | tf_op jit(solution)/shard_map/dot_general | solution.py:102
  57.3 1.6 %collective-permute-start.10 = (f16[2,1,2,64,768]{4,3,2,1,0:T(8,128)(2,1)S(1)}, f16[2,1,2,64,768]{4,3,2,1,0:T(8,128)(2,1)S(1)}, u32[]{:S(2)}, u32[]{:S(2)}) collective-permute-start(f16[2,1,2,64,768]{4,3,2,1,0:T(8,128)(2,1)S(1)} %slice_convert_fusion.2), channel_id=1, source_target_pairs={{0,4},{1,5},{2,6},{3,7},{4,0},{5,1},{6,2},{7,3},{8,12},{9,13},{10,... | collective-permute-start | bytes 1179656 | tf_op jit(solution)/shard_map/ppermute | solution.py:15
  59.0 1.9 %fusion.16 = f32[512,768]{1,0:T(8,128)S(1)} fusion(f32[512,768,1]{1,0,2:T(8,128)S(1)} %fusion.25, bf16[512,2,256]{0,2,1:T(8,128)(2,1)S(1)} %get-tuple-element.31, bf16[2,256,3072]{2,1,0:T(8,128)(2,1)} %collective-permute-done.6, f32[2,256]{1,0:T(2,128)S(1)} %slice.250, f32[2,256]{1,0:T(2,128)S(1)} %slice.248, f32[2,768]{1,0:T(2,128)S(1)} %get-tuple-element.27), kind=kOutput, calls=%fused_computation.25 | convolution fusion | flops 405405696 | bytes 4466688 | tf_op jit(solution)/shard_map/dot_general | solution.py:102
  61.0 1.6 %collective-permute-start.7 = (f16[1,2,2,64,768]{4,3,2,1,0:T(8,128)(2,1)S(1)}, f16[1,2,2,64,768]{4,3,2,1,0:T(8,128)(2,1)S(1)}, u32[]{:S(2)}, u32[]{:S(2)}) collective-permute-start(f16[1,2,2,64,768]{4,3,2,1,0:T(8,128)(2,1)S(1)} %bitcast.136), channel_id=1, source_target_pairs={{0,2},{1,3},{2,0},{3,1},{4,6},{5,7},{6,4},{7,5},{8,10},{9,11},{10,... | collective-permute-start | bytes 1179656 | tf_op jit(solution)/shard_map/ppermute | solution.py:15
  63.4 1.6 %collective-permute-start.17 = (f16[1,1,2,64,768]{4,3,2,1,0:T(8,128)(2,1)S(1)}, f16[1,1,2,64,768]{4,3,2,1,0:T(8,128)(2,1)S(1)}, u32[]{:S(2)}, u32[]{:S(2)}) collective-permute-start(f16[1,1,2,64,768]{4,3,2,1,0:T(8,128)(2,1)S(1)} %slice_convert_fusion.4), channel_id=1, source_target_pairs={{0,4},{1,5},{2,6},{3,7},{4,0},{5,1},{6,2},{7,3},{8,12},{9,13},{10,... | collective-permute-start | bytes 589832 | tf_op jit(solution)/shard_map/ppermute | solution.py:15
  65.0 6.7 %collective-permute-done.13 = f16[1,2,2,64,768]{4,3,2,1,0:T(8,128)(2,1)S(1)} collective-permute-done((f16[1,2,2,64,768]{4,3,2,1,0:T(8,128)(2,1)S(1)}, f16[1,2,2,64,768]{4,3,2,1,0:T(8,128)(2,1)S(1)}, u32[]{:S(2)}, u32[]{:S(2)}) %collective-permute-start.13) | collective-permute-done | bytes 393248 | tf_op jit(solution)/shard_map/ppermute | solution.py:15
  71.8 1.6 %collective-permute-start.14 = (f16[1,1,2,64,768]{4,3,2,1,0:T(8,128)(2,1)S(1)}, f16[1,1,2,64,768]{4,3,2,1,0:T(8,128)(2,1)S(1)}, u32[]{:S(2)}, u32[]{:S(2)}) collective-permute-start(f16[1,1,2,64,768]{4,3,2,1,0:T(8,128)(2,1)S(1)} %slice_convert_fusion.5), channel_id=1, source_target_pairs={{0,4},{1,5},{2,6},{3,7},{4,0},{5,1},{6,2},{7,3},{8,12},{9,13},{10,... | collective-permute-start | bytes 589832 | tf_op jit(solution)/shard_map/ppermute | solution.py:15
  73.6 2.9 %collective-permute-start.11 = (f16[2,1,1,64,768]{4,3,2,1,0:T(8,128)(2,1)S(1)}, f16[2,1,1,64,768]{4,3,2,1,0:T(8,128)(2,1)S(1)}, u32[]{:S(2)}, u32[]{:S(2)}) collective-permute-start(f16[2,1,1,64,768]{4,3,2,1,0:T(8,128)(2,1)S(1)} %slice_convert_fusion.6), channel_id=1, source_target_pairs={{0,8},{1,9},{2,10},{3,11},{4,12},{5,13},{6,14},{7,15},{8,0},{9,1},... | collective-permute-start | bytes 589832 | tf_op jit(solution)/shard_map/ppermute | solution.py:15
  77.8 3.0 %collective-permute-start.18 = (f16[1,1,1,64,768]{4,3,2,1,0:T(8,128)(2,1)S(1)}, f16[1,1,1,64,768]{4,3,2,1,0:T(8,128)(2,1)S(1)}, u32[]{:S(2)}, u32[]{:S(2)}) collective-permute-start(f16[1,1,1,64,768]{4,3,2,1,0:T(8,128)(2,1)S(1)} %slice_convert_fusion.8), channel_id=1, source_target_pairs={{0,8},{1,9},{2,10},{3,11},{4,12},{5,13},{6,14},{7,15},{8,0},{9,1},... | collective-permute-start | bytes 294920 | tf_op jit(solution)/shard_map/ppermute | solution.py:15
  80.8 2.5 %collective-permute-done.14 = f16[1,1,2,64,768]{4,3,2,1,0:T(8,128)(2,1)S(1)} collective-permute-done((f16[1,1,2,64,768]{4,3,2,1,0:T(8,128)(2,1)S(1)}, f16[1,1,2,64,768]{4,3,2,1,0:T(8,128)(2,1)S(1)}, u32[]{:S(2)}, u32[]{:S(2)}) %collective-permute-start.14) | collective-permute-done | bytes 196640 | tf_op jit(solution)/shard_map/ppermute | solution.py:15
  83.6 1.6 %collective-permute-start.12 = (f16[1,1,1,64,768]{4,3,2,1,0:T(8,128)(2,1)S(1)}, f16[1,1,1,64,768]{4,3,2,1,0:T(8,128)(2,1)S(1)}, u32[]{:S(2)}, u32[]{:S(2)}) collective-permute-start(f16[1,1,1,64,768]{4,3,2,1,0:T(8,128)(2,1)S(1)} %slice_convert_fusion.10), channel_id=1, source_target_pairs={{0,2},{1,3},{2,0},{3,1},{4,6},{5,7},{6,4},{7,5},{8,10},{9,11},{10,... | collective-permute-start | bytes 294920 | tf_op jit(solution)/shard_map/ppermute | solution.py:15
  85.6 4.1 %collective-permute-start.9 = (f16[1,1,1,64,768]{4,3,2,1,0:T(8,128)(2,1)S(1)}, f16[1,1,1,64,768]{4,3,2,1,0:T(8,128)(2,1)S(1)}, u32[]{:S(2)}, u32[]{:S(2)}) collective-permute-start(f16[1,1,1,64,768]{4,3,2,1,0:T(8,128)(2,1)S(1)} %slice_convert_fusion.11), channel_id=1, source_target_pairs={{0,8},{1,9},{2,10},{3,11},{4,12},{5,13},{6,14},{7,15},{8,0},{9,1},... | collective-permute-start | bytes 294920 | tf_op jit(solution)/shard_map/ppermute | solution.py:15
  89.7 2.6 %collective-permute-done.15 = f16[1,1,1,64,768]{4,3,2,1,0:T(8,128)(2,1)S(1)} collective-permute-done((f16[1,1,1,64,768]{4,3,2,1,0:T(8,128)(2,1)S(1)}, f16[1,1,1,64,768]{4,3,2,1,0:T(8,128)(2,1)S(1)}, u32[]{:S(2)}, u32[]{:S(2)}) %collective-permute-start.15) | collective-permute-done | bytes 98336 | tf_op jit(solution)/shard_map/ppermute | solution.py:15
  (114 shorter events, 21.4 us)
Async XLA Ops:
  0.0 1.6 %copy-start = (bf16[1024,1024]{1,0:T(8,128)(2,1)S(1)}, bf16[1024,1024]{1,0:T(8,128)(2,1)}, u32[]{:S(2)}) copy-start(bf16[1024,1024]{1,0:T(8,128)(2,1)} %param.6) | copy-start | bytes 6291460
  1.6 4.5 %copy-start.1 = (bf16[2,256,3072]{2,1,0:T(8,128)(2,1)S(1)}, bf16[2,256,3072]{2,1,0:T(8,128)(2,1)}, u32[]{:S(2)}) copy-start(bf16[2,256,3072]{2,1,0:T(8,128)(2,1)} %param.4) | copy-start | bytes 9437188
  5.6 12.2 %collective-permute-start = (bf16[512,1024]{1,0:T(8,128)(2,1)}, bf16[512,1024]{1,0:T(8,128)(2,1)S(1)}, u32[]{:S(2)}, u32[]{:S(2)}) collective-permute-start(bf16[512,1024]{1,0:T(8,128)(2,1)} %fusion.11), channel_id=1, source_target_pairs={{0,1},{1,0},{2,3},{3,2},{4,5},{5,4},{6,7},{7,6},{8,9},{9,8},{10,11... | collective-permute-start | bytes 3145736 | tf_op jit(solution)/shard_map/ppermute | solution.py:15
  7.1 5.8 %collective-permute-start.1 = (f32[2,2,256]{2,1,0:T(2,128)S(1)}, f32[2,2,256]{2,1,0:T(2,128)S(1)}, u32[]{:S(2)}, u32[]{:S(2)}) collective-permute-start(f32[2,2,256]{2,1,0:T(2,128)S(1)} %pad_maximum_fusion.6), channel_id=1, source_target_pairs={{0,16},{16,0},{1,17},{17,1},{2,18},{18,2},{3,19},{19,3},{4,20},{20... | collective-permute-start | bytes 12296 | tf_op jit(solution)/shard_map/ppermute | solution.py:15
  9.8 3.1 %copy-start.2 = (bf16[2,256,3072]{2,1,0:T(8,128)(2,1)S(1)}, bf16[2,256,3072]{2,1,0:T(8,128)(2,1)}, u32[]{:S(2)}) copy-start(bf16[2,256,3072]{2,1,0:T(8,128)(2,1)} %param.4) | copy-start | bytes 9437188
  14.5 3.2 %collective-permute-start.2 = (f32[7168]{0:T(1024)S(1)}, f32[7168]{0:T(1024)S(1)}, u32[]{:S(2)}, u32[]{:S(2)}) collective-permute-start(f32[7168]{0:T(1024)S(1)} %pad_maximum_fusion.4), channel_id=1, source_target_pairs={{0,1},{1,0},{2,3},{3,2},{4,5},{5,4},{6,7},{7,6},{8,9},{9,8},{10,11... | collective-permute-start | bytes 86024 | tf_op jit(solution)/shard_map/ppermute | solution.py:15
  17.8 1.8 %copy-start.8 = (f32[7168]{0:T(1024)}, f32[7168]{0:T(1024)S(1)}, u32[]{:S(2)}) copy-start(f32[7168]{0:T(1024)S(1)} %collective-permute-done.2) | copy-start | bytes 86020
  20.1 4.0 %collective-permute-start.3 = (f32[8192]{0:T(1024)S(1)}, f32[8192]{0:T(1024)S(1)}, u32[]{:S(2)}, u32[]{:S(2)}) collective-permute-start(f32[8192]{0:T(1024)S(1)} %pad_maximum_fusion.1), channel_id=1, source_target_pairs={{0,2},{1,3},{2,0},{3,1},{4,6},{5,7},{6,4},{7,5},{8,10},{9,11},{10,... | collective-permute-start | bytes 98312 | tf_op jit(solution)/shard_map/ppermute | solution.py:15
  22.0 8.8 %copy-start.4 = (f32[512,2]{1,0:T(8,128)}, f32[512,2]{1,0:T(8,128)S(1)}, u32[]{:S(2)}) copy-start(f32[512,2]{1,0:T(8,128)S(1)} %copy.59) | copy-start | bytes 12292
  26.8 4.0 %collective-permute-start.4 = (f32[8192]{0:T(1024)S(1)}, f32[8192]{0:T(1024)S(1)}, u32[]{:S(2)}, u32[]{:S(2)}) collective-permute-start(f32[8192]{0:T(1024)S(1)} %pad_maximum_fusion.2), channel_id=1, source_target_pairs={{0,4},{1,5},{2,6},{3,7},{4,0},{5,1},{6,2},{7,3},{8,12},{9,13},{10,... | collective-permute-start | bytes 98312 | tf_op jit(solution)/shard_map/ppermute | solution.py:15
  28.4 20.7 %collective-permute-start.6 = (bf16[2,256,3072]{2,1,0:T(8,128)(2,1)}, bf16[2,256,3072]{2,1,0:T(8,128)(2,1)}, u32[]{:S(2)}, u32[]{:S(2)}) collective-permute-start(bf16[2,256,3072]{2,1,0:T(8,128)(2,1)} %param.4), channel_id=1, source_target_pairs={{0,1},{1,0},{2,3},{3,2},{4,5},{5,4},{6,7},{7,6},{8,9},{9,8},{10,11... | collective-permute-start | bytes 9437192 | tf_op jit(solution)/shard_map/ppermute | solution.py:15
  30.8 0.6 copy-start.7
  34.9 4.9 %collective-permute-start.5 = (f32[8192]{0:T(1024)S(1)}, f32[8192]{0:T(1024)S(1)}, u32[]{:S(2)}, u32[]{:S(2)}) collective-permute-start(f32[8192]{0:T(1024)S(1)} %pad_maximum_fusion.3), channel_id=1, source_target_pairs={{0,8},{1,9},{2,10},{3,11},{4,12},{5,13},{6,14},{7,15},{8,0},{9,1},... | collective-permute-start | bytes 98312 | tf_op jit(solution)/shard_map/ppermute | solution.py:15
  39.7 0.6 copy-start.6
  40.9 2.8 %copy-start.5 = (f32[512,512]{0,1:T(8,128)S(1)}, f32[512,512]{0,1:T(8,128)}, u32[]{:S(2)}) copy-start(f32[512,512]{0,1:T(8,128)} %get-tuple-element.36) | copy-start | bytes 3145732
  43.7 2.2 %copy-start.3 = (bf16[2,256,3072]{2,1,0:T(8,128)(2,1)S(1)}, bf16[2,256,3072]{2,1,0:T(8,128)(2,1)}, u32[]{:S(2)}) copy-start(bf16[2,256,3072]{2,1,0:T(8,128)(2,1)} %param.4) | copy-start | bytes 9437188
  51.2 12.1 %collective-permute-start.16 = (f16[1,2,2,64,768]{4,3,2,1,0:T(8,128)(2,1)S(1)}, f16[1,2,2,64,768]{4,3,2,1,0:T(8,128)(2,1)S(1)}, u32[]{:S(2)}, u32[]{:S(2)}) collective-permute-start(f16[1,2,2,64,768]{4,3,2,1,0:T(8,128)(2,1)S(1)} %bitcast.138), channel_id=1, source_target_pairs={{0,2},{1,3},{2,0},{3,1},{4,6},{5,7},{6,4},{7,5},{8,10},{9,11},{10,... | collective-permute-start | bytes 1179656 | tf_op jit(solution)/shard_map/ppermute | solution.py:15
  54.8 16.9 %collective-permute-start.13 = (f16[1,2,2,64,768]{4,3,2,1,0:T(8,128)(2,1)S(1)}, f16[1,2,2,64,768]{4,3,2,1,0:T(8,128)(2,1)S(1)}, u32[]{:S(2)}, u32[]{:S(2)}) collective-permute-start(f16[1,2,2,64,768]{4,3,2,1,0:T(8,128)(2,1)S(1)} %bitcast.137), channel_id=1, source_target_pairs={{0,2},{1,3},{2,0},{3,1},{4,6},{5,7},{6,4},{7,5},{8,10},{9,11},{10,... | collective-permute-start | bytes 1179656 | tf_op jit(solution)/shard_map/ppermute | solution.py:15
  57.3 16.1 %collective-permute-start.10 = (f16[2,1,2,64,768]{4,3,2,1,0:T(8,128)(2,1)S(1)}, f16[2,1,2,64,768]{4,3,2,1,0:T(8,128)(2,1)S(1)}, u32[]{:S(2)}, u32[]{:S(2)}) collective-permute-start(f16[2,1,2,64,768]{4,3,2,1,0:T(8,128)(2,1)S(1)} %slice_convert_fusion.2), channel_id=1, source_target_pairs={{0,4},{1,5},{2,6},{3,7},{4,0},{5,1},{6,2},{7,3},{8,12},{9,13},{10,... | collective-permute-start | bytes 1179656 | tf_op jit(solution)/shard_map/ppermute | solution.py:15
  61.0 15.5 %collective-permute-start.7 = (f16[1,2,2,64,768]{4,3,2,1,0:T(8,128)(2,1)S(1)}, f16[1,2,2,64,768]{4,3,2,1,0:T(8,128)(2,1)S(1)}, u32[]{:S(2)}, u32[]{:S(2)}) collective-permute-start(f16[1,2,2,64,768]{4,3,2,1,0:T(8,128)(2,1)S(1)} %bitcast.136), channel_id=1, source_target_pairs={{0,2},{1,3},{2,0},{3,1},{4,6},{5,7},{6,4},{7,5},{8,10},{9,11},{10,... | collective-permute-start | bytes 1179656 | tf_op jit(solution)/shard_map/ppermute | solution.py:15
  63.4 14.4 %collective-permute-start.17 = (f16[1,1,2,64,768]{4,3,2,1,0:T(8,128)(2,1)S(1)}, f16[1,1,2,64,768]{4,3,2,1,0:T(8,128)(2,1)S(1)}, u32[]{:S(2)}, u32[]{:S(2)}) collective-permute-start(f16[1,1,2,64,768]{4,3,2,1,0:T(8,128)(2,1)S(1)} %slice_convert_fusion.4), channel_id=1, source_target_pairs={{0,4},{1,5},{2,6},{3,7},{4,0},{5,1},{6,2},{7,3},{8,12},{9,13},{10,... | collective-permute-start | bytes 589832 | tf_op jit(solution)/shard_map/ppermute | solution.py:15
  71.8 11.6 %collective-permute-start.14 = (f16[1,1,2,64,768]{4,3,2,1,0:T(8,128)(2,1)S(1)}, f16[1,1,2,64,768]{4,3,2,1,0:T(8,128)(2,1)S(1)}, u32[]{:S(2)}, u32[]{:S(2)}) collective-permute-start(f16[1,1,2,64,768]{4,3,2,1,0:T(8,128)(2,1)S(1)} %slice_convert_fusion.5), channel_id=1, source_target_pairs={{0,4},{1,5},{2,6},{3,7},{4,0},{5,1},{6,2},{7,3},{8,12},{9,13},{10,... | collective-permute-start | bytes 589832 | tf_op jit(solution)/shard_map/ppermute | solution.py:15
  73.6 10.0 %collective-permute-start.11 = (f16[2,1,1,64,768]{4,3,2,1,0:T(8,128)(2,1)S(1)}, f16[2,1,1,64,768]{4,3,2,1,0:T(8,128)(2,1)S(1)}, u32[]{:S(2)}, u32[]{:S(2)}) collective-permute-start(f16[2,1,1,64,768]{4,3,2,1,0:T(8,128)(2,1)S(1)} %slice_convert_fusion.6), channel_id=1, source_target_pairs={{0,8},{1,9},{2,10},{3,11},{4,12},{5,13},{6,14},{7,15},{8,0},{9,1},... | collective-permute-start | bytes 589832 | tf_op jit(solution)/shard_map/ppermute | solution.py:15
  76.6 8.9 %collective-permute-start.8 = (f16[1,1,2,64,768]{4,3,2,1,0:T(8,128)(2,1)S(1)}, f16[1,1,2,64,768]{4,3,2,1,0:T(8,128)(2,1)S(1)}, u32[]{:S(2)}, u32[]{:S(2)}) collective-permute-start(f16[1,1,2,64,768]{4,3,2,1,0:T(8,128)(2,1)S(1)} %slice_convert_fusion.7), channel_id=1, source_target_pairs={{0,4},{1,5},{2,6},{3,7},{4,0},{5,1},{6,2},{7,3},{8,12},{9,13},{10,... | collective-permute-start | bytes 589832 | tf_op jit(solution)/shard_map/ppermute | solution.py:15
  77.8 11.8 %collective-permute-start.18 = (f16[1,1,1,64,768]{4,3,2,1,0:T(8,128)(2,1)S(1)}, f16[1,1,1,64,768]{4,3,2,1,0:T(8,128)(2,1)S(1)}, u32[]{:S(2)}, u32[]{:S(2)}) collective-permute-start(f16[1,1,1,64,768]{4,3,2,1,0:T(8,128)(2,1)S(1)} %slice_convert_fusion.8), channel_id=1, source_target_pairs={{0,8},{1,9},{2,10},{3,11},{4,12},{5,13},{6,14},{7,15},{8,0},{9,1},... | collective-permute-start | bytes 294920 | tf_op jit(solution)/shard_map/ppermute | solution.py:15
  83.5 8.8 %collective-permute-start.15 = (f16[1,1,1,64,768]{4,3,2,1,0:T(8,128)(2,1)S(1)}, f16[1,1,1,64,768]{4,3,2,1,0:T(8,128)(2,1)S(1)}, u32[]{:S(2)}, u32[]{:S(2)}) collective-permute-start(f16[1,1,1,64,768]{4,3,2,1,0:T(8,128)(2,1)S(1)} %slice_convert_fusion.9), channel_id=1, source_target_pairs={{0,8},{1,9},{2,10},{3,11},{4,12},{5,13},{6,14},{7,15},{8,0},{9,1},... | collective-permute-start | bytes 294920 | tf_op jit(solution)/shard_map/ppermute | solution.py:15
  83.6 8.7 %collective-permute-start.12 = (f16[1,1,1,64,768]{4,3,2,1,0:T(8,128)(2,1)S(1)}, f16[1,1,1,64,768]{4,3,2,1,0:T(8,128)(2,1)S(1)}, u32[]{:S(2)}, u32[]{:S(2)}) collective-permute-start(f16[1,1,1,64,768]{4,3,2,1,0:T(8,128)(2,1)S(1)} %slice_convert_fusion.10), channel_id=1, source_target_pairs={{0,2},{1,3},{2,0},{3,1},{4,6},{5,7},{6,4},{7,5},{8,10},{9,11},{10,... | collective-permute-start | bytes 294920 | tf_op jit(solution)/shard_map/ppermute | solution.py:15
  85.6 7.8 %collective-permute-start.9 = (f16[1,1,1,64,768]{4,3,2,1,0:T(8,128)(2,1)S(1)}, f16[1,1,1,64,768]{4,3,2,1,0:T(8,128)(2,1)S(1)}, u32[]{:S(2)}, u32[]{:S(2)}) collective-permute-start(f16[1,1,1,64,768]{4,3,2,1,0:T(8,128)(2,1)S(1)} %slice_convert_fusion.11), channel_id=1, source_target_pairs={{0,8},{1,9},{2,10},{3,11},{4,12},{5,13},{6,14},{7,15},{8,0},{9,1},... | collective-permute-start | bytes 294920 | tf_op jit(solution)/shard_map/ppermute | solution.py:15

commit v2 on v1

v2 whole, which is shorter than its diff:
```python
import functools
import math

import jax
import jax.numpy as jnp
from jax import lax
from jax.experimental import pallas as pl
from jax.experimental.pallas import tpu as pltpu
from jax.sharding import PartitionSpec as P

EPSILON = 1e-06
LIFT = 256.0
LANES = 128
ROWS = 8
CHUNKS = ((1024, False), (512, True), (1024, False), (512, False))
IN_VMEM = pl.BlockSpec(memory_space=pltpu.VMEM)


def call(body, out_shapes, args, flops=0, moved=0, **kw):
    return pl.pallas_call(
        body,
        out_shape=[jax.ShapeDtypeStruct(s, t) for s, t in out_shapes],
        cost_estimate=pl.CostEstimate(flops=flops, bytes_accessed=moved, transcendentals=0),
        compiler_params=pltpu.CompilerParams(vmem_limit_bytes=48 << 20),
        **kw,
    )(*args)


def swap(value, axis, bit):
    size = lax.axis_size(axis)
    return lax.ppermute(value, axis, [(d, d ^ bit) for d in range(size)])


def fold_lanes(tile):
    total = tile[:, :LANES]
    for start in range(LANES, tile.shape[1], LANES):
        total = total + tile[:, start : start + LANES]
    return total


def as_row(partial):
    return jnp.sum(partial.T, axis=0, keepdims=True)


def as_column(row):
    return jnp.broadcast_to(row, (LANES, LANES)).T


def token_sums_body(x_ref, out_ref):
    values = x_ref[0].astype(jnp.float32)
    first = as_row(fold_lanes(values))
    second = as_row(fold_lanes(values * values))
    out_ref[...] = jnp.concatenate(
        [first, second, jnp.zeros((ROWS - 2, first.shape[1]), jnp.float32)], axis=0
    )


def token_sums(x):
    mb, tok, width = x.shape
    per = tok // LANES
    return pl.pallas_call(
        token_sums_body,
        grid=(mb * per,),
        in_specs=[pl.BlockSpec((1, LANES, width), lambda i: (i // per, i % per, 0))],
        out_specs=pl.BlockSpec((ROWS, LANES), lambda i: (0, i)),
        out_shape=jax.ShapeDtypeStruct((ROWS, mb * tok), jnp.float32),
        cost_estimate=pl.CostEstimate(flops=4 * x.size, bytes_accessed=2 * x.size, transcendentals=0),
    )(x)


def moments(sums, count):
    mean = sums[0:1] / count
    return mean, lax.rsqrt(sums[1:2] / count - mean * mean + EPSILON)


def power_body(count, x_ref, mine_ref, theirs_ref, out_ref, acc_ref):
    mb = pl.program_id(0)
    block = pl.program_id(1)
    per = pl.num_programs(1)
    width = x_ref.shape[2]
    sums = mine_ref[0:2, :] + theirs_ref[0:2, :]
    mean, rstd = moments(sums, count)
    mean, rstd = as_column(mean), as_column(rstd)

    @pl.when(block == 0)
    def _():
        acc_ref[...] = jnp.zeros_like(acc_ref)

    for start in range(0, width, LANES):
        values = x_ref[0, :, start : start + LANES].astype(jnp.float32)
        normed = (values - mean) * rstd
        square = (normed * normed).reshape(LANES // ROWS, ROWS, LANES)
        acc_ref[:, start : start + LANES] += jnp.sum(square, axis=0)

    quarter = ROWS // 2
    size = width // quarter

    @pl.when(block == per - 1)
    def _():
        line = jnp.sum(acc_ref[...], axis=0, keepdims=True)
        for m in range(2):

            @pl.when(mb == m)
            def _():
                for q in range(quarter):
                    out_ref[m * quarter + q : m * quarter + q + 1, :size] = line[:, q * size : (q + 1) * size]

    for stat in range(2):
        for m in range(2):
            for b in range(ROWS // 4):

                @pl.when((mb == m) & (block == b))
                def _():
                    r = stat * (ROWS // 2) + m * (ROWS // 4) + b
                    out_ref[r : r + 1, size:] = sums[stat : stat + 1, :]


def power_sums(x, mine, theirs, count):
    mb, tok, width = x.shape
    per = tok // LANES
    assert mb == 2 and per * 2 == ROWS // 2
    token = pl.BlockSpec((ROWS, LANES), lambda m, i: (0, m * per + i))
    shape = (ROWS, width // (ROWS // 2) + LANES)
    return pl.pallas_call(
        functools.partial(power_body, count),
        grid=(mb, per),
        in_specs=[pl.BlockSpec((1, LANES, width), lambda m, i: (m, i, 0)), token, token],
        out_specs=pl.BlockSpec(shape, lambda m, i: (0, 0)),
        out_shape=jax.ShapeDtypeStruct(shape, jnp.float32),
        scratch_shapes=[pltpu.VMEM((ROWS, width), jnp.float32)],
        cost_estimate=pl.CostEstimate(flops=5 * x.size, bytes_accessed=2 * x.size, transcendentals=0),
    )(x, mine, theirs)


def project_body(mb, sel_ref, own_ref, partner_ref, proj_ref, sums_ref):
    feats = sel_ref.shape[0]
    tok = own_ref.shape[0] // mb
    for side, ref in enumerate((own_ref, partner_ref)):
        proj_ref[:, side * mb * tok : (side + 1) * mb * tok] = lax.dot_general(
            sel_ref[...], ref[...], (((1,), (1,)), ((), ())), preferred_element_type=jnp.float32
        )
    half = feats // 2
    for m in range(mb):
        pieces = [proj_ref[:, (side * mb + m) * tok : (side * mb + m + 1) * tok] for side in range(2)]
        one = as_row(fold_lanes(pieces[0]) + fold_lanes(pieces[1]))
        two = as_row(fold_lanes(pieces[0] * pieces[0]) + fold_lanes(pieces[1] * pieces[1]))
        for stat, line in enumerate((one, two)):
            r = (stat * mb + m) * 2
            sums_ref[r : r + 1, :] = line[:, :half]
            sums_ref[r + 1 : r + 2, :] = line[:, half:]


def join_body(power_ref, got_ref, sums_ref, out_ref):
    size = power_ref.shape[1] - LANES
    out_ref[:, :size] = power_ref[:, :size] + got_ref[:, :size]
    out_ref[:, size:] = sums_ref[...]


def hop_body(stride, half, mine_ref, got_ref, out_ref):
    size = out_ref.shape[1] - half
    out_ref[:, :size] = mine_ref[:, :size] + got_ref[:, :size]
    theirs = got_ref[:, size:]
    if stride >= half:
        row = lax.broadcasted_iota(jnp.int32, theirs.shape, 0)
        theirs = jnp.where(row % 2 == 1, pltpu.roll(theirs, 1, 0), pltpu.roll(theirs, ROWS - 1, 0))
    else:
        lane = lax.broadcasted_iota(jnp.int32, theirs.shape, 1)
        theirs = jnp.where(
            (lane & stride) != 0, pltpu.roll(theirs, stride, 1), pltpu.roll(theirs, half - stride, 1)
        )
    out_ref[:, size:] = mine_ref[:, size:] + theirs


def student_body(mb, total, proj_ref, hop_ref, own_ref, partner_ref, scale_ref):
    feats = proj_ref.shape[0]
    half = feats // 2
    size = hop_ref.shape[1] - half
    tok = own_ref.shape[1] // mb
    quarter = ROWS // mb
    for m in range(mb):
        for q in range(quarter):
            scale_ref[m : m + 1, q * size : (q + 1) * size] = lax.rsqrt(
                hop_ref[m * quarter + q : m * quarter + q + 1, :size] / total + EPSILON
            )
        for block in range(feats // LANES):
            rows = slice(block * LANES, (block + 1) * LANES)
            part, lane = divmod(block * LANES, half)
            lines = []
            for stat in range(2):
                r = (stat * mb + m) * 2 + part
                lines.append(hop_ref[r : r + 1, size + lane : size + lane + LANES] / total)
            spread = lax.rsqrt(lines[1] - lines[0] * lines[0] + EPSILON)
            mean, spread = as_column(lines[0]), as_column(spread)
            for side, ref in enumerate((own_ref, partner_ref)):
                for start in range(0, tok, LANES):
                    at = (side * mb + m) * tok + start
                    ref[rows, m * tok + start : m * tok + start + LANES] = (
                        (proj_ref[rows, at : at + LANES] - mean) * spread
                    ).astype(jnp.bfloat16)


def columns_body(count, mine_ref, theirs_ref, packed_ref, mean_ref, rstd_ref):
    tokens = mine_ref.shape[1]
    size = packed_ref.shape[1] - LANES
    for block in range(tokens // LANES):
        sums = (
            mine_ref[0:2, block * LANES : (block + 1) * LANES]
            + theirs_ref[0:2, block * LANES : (block + 1) * LANES]
        )
        other = jnp.concatenate(
            [packed_ref[block : block + 1, size:], packed_ref[block + ROWS // 2 : block + ROWS // 2 + 1, size:]],
            axis=0,
        )
        for side, pair in enumerate((sums, other)):
            mean, rstd = moments(pair, count)
            at = side * tokens + block * LANES
            mean_ref[at : at + LANES, :] = as_column(mean)
            rstd_ref[at : at + LANES, :] = as_column(rstd)


def product_body(
    mb, start, width, factor, own_z, partner_z, own_x, partner_x, mean_ref, rstd_ref, scale_ref, keep_ref, send_ref, tz_ref
):
    tokens = own_z.shape[1]
    tok = tokens // mb
    total = None
    for side, (z_ref, x_ref) in enumerate(((own_z, own_x), (partner_z, partner_x))):
        for m in range(mb):
            for block in range(tok // LANES):
                at = m * tok + block * LANES
                mean = mean_ref[side * tokens + at : side * tokens + at + LANES, :]
                rstd = rstd_ref[side * tokens + at : side * tokens + at + LANES, :]
                for c in range(0, width, LANES):
                    values = x_ref[
                        m, block * LANES : (block + 1) * LANES, start + c : start + c + LANES
                    ].astype(jnp.float32)
                    tz_ref[side, at : at + LANES, c : c + LANES] = (
                        (values - mean) * rstd * scale_ref[m : m + 1, start + c : start + c + LANES]
                    ).astype(jnp.bfloat16)
    half = own_z.shape[0] // 2
    for part, ref in ((1, send_ref), (0, keep_ref)):
        rows = slice(part * half, (part + 1) * half)
        total = jnp.dot(own_z[rows, :], tz_ref[0], preferred_element_type=jnp.float32)
        total = total + jnp.dot(partner_z[rows, :], tz_ref[1], preferred_element_type=jnp.float32)
        ref[...] = total * factor


def shards(teacher, features, w_first, w_second):
    mb, tok, width = teacher.shape
    ds = w_second.shape[1]
    n = lax.axis_size("dp")
    grp = lax.axis_size("grp")
    me = lax.axis_index("dp")
    hops = n.bit_length() - 2
    rows = ds // n
    token_total = tok * n
    blocks = n // 2
    feats = blocks * rows
    half = feats // 2
    tokens = mb * tok
    count = width * grp

    partner_x = swap(teacher, "dp", 1)
    mine = token_sums(teacher)
    theirs = swap(mine, "grp", 1)

    hidden = jax.nn.gelu(
        jnp.dot(features.reshape(tokens, -1), w_first, preferred_element_type=jnp.float32)
    ).astype(jnp.bfloat16)
    partner_hidden = swap(hidden, "dp", 1)

    index = jnp.arange(blocks)
    distance = jnp.zeros_like(index)
    for h in range(hops):
        distance = distance + (((index >> (hops - 1 - h)) & 1) << (h + 1))
    owner = me ^ distance
    source = (owner[:, None] * rows + jnp.arange(rows)[None, :]).reshape(-1)
    select = (source[:, None] == jnp.arange(ds)[None, :]).astype(jnp.bfloat16)
    w_sel = lax.dot_general(
        select, w_second, (((1,), (1,)), ((), ())), preferred_element_type=jnp.float32
    ).astype(jnp.bfloat16)

    power = power_sums(teacher, mine, theirs, count)
    got = swap(power, "dp", 1)
    proj, student = call(
        functools.partial(project_body, mb),
        [((feats, 2 * tokens), jnp.float32), ((ROWS, half), jnp.float32)],
        (w_sel, hidden, partner_hidden),
        flops=4 * feats * tokens * ds,
        moved=8 * feats * tokens,
    )
    (total,) = call(join_body, [((ROWS, power.shape[1] - LANES + half), jnp.float32)], (power, got, student))
    mean_b, rstd_b = call(
        functools.partial(columns_body, count),
        [((2 * tokens, LANES), jnp.float32)] * 2,
        (mine, theirs, got),
        moved=8 * tokens * LANES,
    )
    for h in range(hops):
        (total,) = call(
            functools.partial(hop_body, feats >> (h + 1), half),
            [(total.shape, jnp.float32)],
            (total, swap(total, "dp", 2 << h)),
        )
    own_z, partner_z, scale = call(
        functools.partial(student_body, mb, token_total),
        [((feats, tokens), jnp.bfloat16)] * 2 + [((mb, width), jnp.float32)],
        (proj, total),
        moved=8 * feats * tokens,
    )
    factor = LIFT / math.sqrt(mb * token_total)

    bits = (2,) * (hops - 1)
    pieces = []
    start = 0
    for size, late in CHUNKS:
        keep, send = pl.pallas_call(
            functools.partial(product_body, mb, start, size, factor),
            out_shape=[jax.ShapeDtypeStruct((half, size), jnp.float32)] * 2,
            scratch_shapes=[pltpu.VMEM((2, tokens, size), jnp.bfloat16)],
            cost_estimate=pl.CostEstimate(
                flops=4 * feats * tokens * size, bytes_accessed=4 * feats * size, transcendentals=0
            ),
            compiler_params=pltpu.CompilerParams(vmem_limit_bytes=48 << 20),
        )(own_z, partner_z, teacher, partner_x, mean_b, rstd_b, scale)
        start += size
        keep = keep.reshape((1,) + bits + (rows, size))
        send = send.reshape((1,) + bits + (rows, size))
        if late:
            held = jnp.concatenate([keep, send], axis=0)
        else:
            held = keep + swap(send.astype(jnp.float16), "dp", 2).astype(jnp.float32)
        order = list(range(1, hops)) + ([0] if late else [])
        for h in order:
            kept = lax.index_in_dim(held, 0, h, keepdims=True)
            sent = lax.index_in_dim(held, 1, h, keepdims=True).astype(jnp.float16)
            held = kept + swap(sent, "dp", 2 << h).astype(jnp.float32)
        pieces.append(held.reshape(rows, size) * (1.0 / LIFT))
    return jnp.concatenate(pieces, axis=1)


def solution(mesh):
    placed = (P(None, "dp", "grp"), P(None, "dp", None), P(), P())
    return jax.shard_map(
        shards, mesh=mesh, in_specs=placed, out_specs=P("dp", "grp"), check_vma=False
    )
```

time: 95.9 us -> 95.3 us (level); the launches traced: 94.3 us -> 94.9 us
  Pallas kernels: 0 us -> 29 us
  matrix products: 22.7 us -> 6.77 us
  other arithmetic: 10.2 us -> 2.19 us
  local copies, waits for them, and re-layouts: 10.8 us -> 3.01 us
  waiting for transfers between devices: 19.6 us -> 24.3 us
  starting transfers between devices: 30.6 us -> 29.4 us
    pallas_call x0 -> x13, Pallas kernels: none -> 29 us  [the longest x4 16.9 us: shards(): pl.pallas_call(functools.partial(product_body, mb, start, size, factor),...]
    dot_general x11 -> x1, matrix products: 19.6 us -> 2.86 us  [shards(): jnp.dot(features.reshape(tokens, -1), w_first, preferred_element_type=jnp...]
    ppermute x19, waiting for transfers between devices: 19.6 us -> 24.3 us  [swap(): return lax.ppermute(value, axis, [(d, d ^ bit) for d in range(size)])]
    reshape x6 -> x0, local copies, waits for them, and re-layouts: 4.04 us -> none  [the longest x3 2.2 us: shards(): theirs = got[count:].reshape((2,) + bits + (rows, mb))]
    reduce_sum x2 -> x0, other arithmetic: 2.54 us -> none  [the longest x1 1.53 us: shards(): power = jnp.sum(normed * normed, axis=1)]
    add x14 -> x8, other arithmetic: 2.77 us -> 0.66 us  [the longest x3 0.37 us: shards(): held = keep + swap(send.astype(jnp.float16), 'dp', 2).astype(jnp.float32)]
    slice x11 -> x0, local copies, waits for them, and re-layouts: 1.61 us -> none  [the longest x4 0.81 us: shards(): power = power + got[:count]]
    convert_element_type x1 -> x3, other arithmetic: 1.67 us -> 0.19 us  [shards(): held = keep + swap(send.astype(jnp.float16), 'dp', 2).astype(jnp.float32)]
  transfers between devices with their start and end apart: 19 -> 19, of which waited for: 9 -> 10; matrix products, arithmetic and copies ran while one was open for 30% -> 8% of each run, Pallas kernels for 0% -> 26%
where the time goes in v2:
time: 95.3 us; the launch traced here: 94.9 us
  starting transfers between devices  29.4 us (31%)
  Pallas kernels  29 us (30%)
  waiting for transfers between devices  24.3 us (25%)
  matrix products  6.77 us (7%)
  local copies, waits for them, and re-layouts  3.01 us (3%)
  other arithmetic  2.19 us (2%)
    ppermute x19, starting transfers between devices, swap(): return lax.ppermute(value, axis, [(d, d ^ bit) for d in range(size)])  29.4 us
    ppermute x19, waiting for transfers between devices, swap(): return lax.ppermute(value, axis, [(d, d ^ bit) for d in range(size)])  24.3 us
    pallas_call x4, Pallas kernels, shards(): pl.pallas_call(functools.partial(product_body, mb, start, size, factor),...  16.9 us
    pallas_call x1, Pallas kernels, power_sums(): pl.pallas_call(functools.partial(power_body, count), grid=(mb, per), in_s...  4.3 us
    pallas_call x1, Pallas kernels, token_sums(): pl.pallas_call(token_sums_body, grid=(mb * per,), in_specs=[pl.BlockSpec(...  4.07 us
    dot_general x1, matrix products, shards(): lax.dot_general(select, w_second, (((1,), (1,)), ((), ())), preferred_ele...  3.9 us
    pallas_call x7, Pallas kernels, call(): pl.pallas_call(body, out_shape=[jax.ShapeDtypeStruct(s, t) for s, t in ou...  3.65 us
    unnamed x12, local copies, waits for them, and re-layouts  2.93 us
  transfers between devices with their start and end apart: 19, of which 10 were waited for; matrix products, arithmetic and copies ran while one was open for 8% of the time, Pallas kernels for 26%

profile of v2, /device:TPU:0, one launch (start us, length us, event | category | flops | bytes accessed | tf_op | source)
XLA Modules:
  0.0 94.9 jit_solution(16484885447521327281)
XLA Ops:
  0.5 1.1 %copy-done = bf16[1024,1024]{1,0:T(8,128)(2,1)S(1)} copy-done((bf16[1024,1024]{1,0:T(8,128)(2,1)S(1)}, bf16[1024,1024]{1,0:T(8,128)(2,1)}, u32[]{:S(2)}) %copy-start) | copy-done | bytes 2097176
  1.6 2.9 %fusion.7.own_ref = bf16[512,1024]{1,0:T(8,128)(2,1)S(1)} fusion(bf16[512,1024]{1,0:T(8,128)(2,1)} %bitcast.30, bf16[1024,1024]{1,0:T(8,128)(2,1)S(1)} %copy-done), kind=kOutput, calls=%fused_computation.8 | convolution fusion | flops 1078460416 | bytes 4194304 | tf_op jit(solution)/shard_map/dot_general | solution.py:268
  5.0 4.1 %shard_map.47.mine_ref = f32[8,512]{1,0:T(8,128)} custom-call(bf16[2,256,3072]{2,1,0:T(8,128)(2,1)} %own_x.7), custom_call_target="tpu_custom_call" | custom-call | flops 6291456 | bytes 3145728 | tf_op jit(solution)/shard_map/pallas_call | solution.py:61
  9.1 2.5 %collective-permute-start.1 = (f32[8,512]{1,0:T(8,128)}, f32[8,512]{1,0:T(8,128)S(1)}, u32[]{:S(2)}, u32[]{:S(2)}) collective-permute-start(f32[8,512]{1,0:T(8,128)} %shard_map.47.mine_ref), channel_id=1, source_target_pairs={{0,16},{16,0},{1,17},{17,1},{2,18},{18,2},{3,19},{19,3},{4,20},{20... | collective-permute-start | bytes 49160 | tf_op jit(solution)/shard_map/ppermute | solution.py:31
  11.8 3.9 %fusion.9.sel_ref = bf16[512,1024]{1,0:T(8,128)(2,1)} fusion(bf16[1024,1024]{1,0:T(8,128)(2,1)} %param.7, s32[512]{0:T(512)S(1)} %add.84), kind=kOutput, calls=%fused_computation.11 | convolution fusion | flops 1074790400 | bytes 3147776 | tf_op jit(solution)/shard_map/dot_general | solution.py:279
  16.3 4.3 %shard_map.48.power_ref = f32[8,896]{1,0:T(8,128)} custom-call(bf16[2,256,3072]{2,1,0:T(8,128)(2,1)} %own_x.7, f32[8,512]{1,0:T(8,128)} %shard_map.47.mine_ref, f32[8,512]{1,0:T(8,128)} %copy-done.3), custom_call_target="tpu_custom_call" | custom-call | flops 7864320 | bytes 3145728 | tf_op jit(solution)/shard_map/pallas_call | solution.py:124
  20.9 1.2 %copy-done.5 = bf16[512,1024]{1,0:T(8,128)(2,1)S(1)} copy-done((bf16[512,1024]{1,0:T(8,128)(2,1)S(1)}, bf16[512,1024]{1,0:T(8,128)(2,1)}, u32[]{:S(2)}) %copy-start.5) | copy-done | bytes 1048600
  22.1 2.9 %shard_map.46 = (f32[512,1024]{1,0:T(8,128)S(1)}, f32[8,256]{1,0:T(8,128)S(1)}) custom-call(bf16[512,1024]{1,0:T(8,128)(2,1)S(1)} %copy-done.5, bf16[512,1024]{1,0:T(8,128)(2,1)S(1)} %fusion.7.own_ref, bf16[512,1024]{1,0:T(8,128)(2,1)} %collective-permute-done.partner_ref), custom_call_target="tpu_custom_call" | custom-call | flops 1073741824 | bytes 2097152 | tf_op jit(solution)/shard_map/pallas_call | solution.py:20
  25.0 1.6 %collective-permute-start.3 = (f32[8,1024]{1,0:T(8,128)S(1)}, f32[8,1024]{1,0:T(8,128)S(1)}, u32[]{:S(2)}, u32[]{:S(2)}) collective-permute-start(f32[8,1024]{1,0:T(8,128)S(1)} %shard_map.49.mine_ref), channel_id=1, source_target_pairs={{0,2},{1,3},{2,0},{3,1},{4,6},{5,7},{6,4},{7,5},{8,10},{9,11},{10,... | collective-permute-start | bytes 98312 | tf_op jit(solution)/shard_map/ppermute | solution.py:31
  26.6 2.4 %collective-permute-done.3.got_ref = f32[8,1024]{1,0:T(8,128)S(1)} collective-permute-done((f32[8,1024]{1,0:T(8,128)S(1)}, f32[8,1024]{1,0:T(8,128)S(1)}, u32[]{:S(2)}, u32[]{:S(2)}) %collective-permute-start.3) | collective-permute-done | bytes 32800 | tf_op jit(solution)/shard_map/ppermute | solution.py:31
  29.0 1.6 %collective-permute-start.4 = (f32[8,1024]{1,0:T(8,128)S(1)}, f32[8,1024]{1,0:T(8,128)S(1)}, u32[]{:S(2)}, u32[]{:S(2)}) collective-permute-start(f32[8,1024]{1,0:T(8,128)S(1)} %shard_map.50.mine_ref), channel_id=1, source_target_pairs={{0,4},{1,5},{2,6},{3,7},{4,0},{5,1},{6,2},{7,3},{8,12},{9,13},{10,... | collective-permute-start | bytes 98312 | tf_op jit(solution)/shard_map/ppermute | solution.py:31
  30.6 2.3 %collective-permute-done.4.got_ref = f32[8,1024]{1,0:T(8,128)S(1)} collective-permute-done((f32[8,1024]{1,0:T(8,128)S(1)}, f32[8,1024]{1,0:T(8,128)S(1)}, u32[]{:S(2)}, u32[]{:S(2)}) %collective-permute-start.4) | collective-permute-done | bytes 32800 | tf_op jit(solution)/shard_map/ppermute | solution.py:31
  33.0 2.6 %collective-permute-start.5 = (f32[8,1024]{1,0:T(8,128)S(1)}, f32[8,1024]{1,0:T(8,128)S(1)}, u32[]{:S(2)}, u32[]{:S(2)}) collective-permute-start(f32[8,1024]{1,0:T(8,128)S(1)} %shard_map.51.mine_ref), channel_id=1, source_target_pairs={{0,8},{1,9},{2,10},{3,11},{4,12},{5,13},{6,14},{7,15},{8,0},{9,1},... | collective-permute-start | bytes 98312 | tf_op jit(solution)/shard_map/ppermute | solution.py:31
  35.9 1.9 %collective-permute-done.5.got_ref = f32[8,1024]{1,0:T(8,128)S(1)} collective-permute-done((f32[8,1024]{1,0:T(8,128)S(1)}, f32[8,1024]{1,0:T(8,128)S(1)}, u32[]{:S(2)}, u32[]{:S(2)}) %collective-permute-start.5) | collective-permute-done | bytes 32800 | tf_op jit(solution)/shard_map/ppermute | solution.py:31
  38.2 3.8 %shard_map.58 = (f32[256,512]{1,0:T(8,128)S(1)}, f32[256,512]{1,0:T(8,128)S(1)}) custom-call(bf16[512,512]{1,0:T(8,128)(2,1)S(1)} %get-tuple-element.22.own_z, bf16[512,512]{1,0:T(8,128)(2,1)S(1)} %get-tuple-element.23.partner_z, bf16[2,256,3072]{2,1,0:T(8,128)(2,1)} %own_x.7, bf16[2,256,3072]{2,1,0:T(8,128)(2,1)} %collective-permute-done.6.partner_x, ...), custom_call_target="tpu_custom_call" | custom-call | flops 536870912 | bytes 1048576 | tf_op jit(solution)/shard_map/pallas_call | solution.py:317
  42.1 1.6 %collective-permute-start.16 = (f16[1,2,2,64,512]{4,3,2,1,0:T(8,128)(2,1)S(1)}, f16[1,2,2,64,512]{4,3,2,1,0:T(8,128)(2,1)S(1)}, u32[]{:S(2)}, u32[]{:S(2)}) collective-permute-start(f16[1,2,2,64,512]{4,3,2,1,0:T(8,128)(2,1)S(1)} %bitcast.29), channel_id=1, source_target_pairs={{0,2},{1,3},{2,0},{3,1},{4,6},{5,7},{6,4},{7,5},{8,10},{9,11},{10,... | collective-permute-start | bytes 786440 | tf_op jit(solution)/shard_map/ppermute | solution.py:31
  43.7 4.7 %shard_map.57 = (f32[256,1024]{1,0:T(8,128)S(1)}, f32[256,1024]{1,0:T(8,128)S(1)}) custom-call(bf16[512,512]{1,0:T(8,128)(2,1)S(1)} %get-tuple-element.22.own_z, bf16[512,512]{1,0:T(8,128)(2,1)S(1)} %get-tuple-element.23.partner_z, bf16[2,256,3072]{2,1,0:T(8,128)(2,1)} %own_x.7, bf16[2,256,3072]{2,1,0:T(8,128)(2,1)} %collective-permute-done.6.partner_x, ...), custom_call_target="tpu_custom_call" | custom-call | flops 1073741824 | bytes 2097152 | tf_op jit(solution)/shard_map/pallas_call | solution.py:317
  49.0 3.8 %shard_map.56 = (f32[256,512]{1,0:T(8,128)S(1)}, f32[256,512]{1,0:T(8,128)S(1)}) custom-call(bf16[512,512]{1,0:T(8,128)(2,1)S(1)} %get-tuple-element.22.own_z, bf16[512,512]{1,0:T(8,128)(2,1)S(1)} %get-tuple-element.23.partner_z, bf16[2,256,3072]{2,1,0:T(8,128)(2,1)} %own_x.7, bf16[2,256,3072]{2,1,0:T(8,128)(2,1)} %collective-permute-done.6.partner_x, ...), custom_call_target="tpu_custom_call" | custom-call | flops 536870912 | bytes 1048576 | tf_op jit(solution)/shard_map/pallas_call | solution.py:317
  52.9 1.6 %collective-permute-start.10 = (f16[2,1,2,64,512]{4,3,2,1,0:T(8,128)(2,1)S(1)}, f16[2,1,2,64,512]{4,3,2,1,0:T(8,128)(2,1)S(1)}, u32[]{:S(2)}, u32[]{:S(2)}) collective-permute-start(f16[2,1,2,64,512]{4,3,2,1,0:T(8,128)(2,1)S(1)} %fusion.13), channel_id=1, source_target_pairs={{0,4},{1,5},{2,6},{3,7},{4,0},{5,1},{6,2},{7,3},{8,12},{9,13},{10,... | collective-permute-start | bytes 786440 | tf_op jit(solution)/shard_map/ppermute | solution.py:31
  54.5 4.7 %shard_map.55 = (f32[256,1024]{1,0:T(8,128)S(1)}, f32[256,1024]{1,0:T(8,128)S(1)}) custom-call(bf16[512,512]{1,0:T(8,128)(2,1)S(1)} %get-tuple-element.22.own_z, bf16[512,512]{1,0:T(8,128)(2,1)S(1)} %get-tuple-element.23.partner_z, bf16[2,256,3072]{2,1,0:T(8,128)(2,1)} %own_x.7, bf16[2,256,3072]{2,1,0:T(8,128)(2,1)} %collective-permute-done.6.partner_x, ...), custom_call_target="tpu_custom_call" | custom-call | flops 1073741824 | bytes 2097152 | tf_op jit(solution)/shard_map/pallas_call | solution.py:317
  59.3 1.6 %collective-permute-start.7 = (f16[1,2,2,64,1024]{4,3,2,1,0:T(8,128)(2,1)S(1)}, f16[1,2,2,64,1024]{4,3,2,1,0:T(8,128)(2,1)S(1)}, u32[]{:S(2)}, u32[]{:S(2)}) collective-permute-start(f16[1,2,2,64,1024]{4,3,2,1,0:T(8,128)(2,1)S(1)} %bitcast.28), channel_id=1, source_target_pairs={{0,2},{1,3},{2,0},{3,1},{4,6},{5,7},{6,4},{7,5},{8,10},{9,11},{10,... | collective-permute-start | bytes 1572872 | tf_op jit(solution)/shard_map/ppermute | solution.py:31
  61.6 2.7 %collective-permute-start.11 = (f16[2,1,1,64,512]{4,3,2,1,0:T(8,128)(2,1)S(1)}, f16[2,1,1,64,512]{4,3,2,1,0:T(8,128)(2,1)S(1)}, u32[]{:S(2)}, u32[]{:S(2)}) collective-permute-start(f16[2,1,1,64,512]{4,3,2,1,0:T(8,128)(2,1)S(1)} %slice_convert_fusion.4), channel_id=1, source_target_pairs={{0,8},{1,9},{2,10},{3,11},{4,12},{5,13},{6,14},{7,15},{8,0},{9,1},... | collective-permute-start | bytes 393224 | tf_op jit(solution)/shard_map/ppermute | solution.py:31
  64.3 1.9 %collective-permute-done.17 = f16[1,1,2,64,512]{4,3,2,1,0:T(8,128)(2,1)S(1)} collective-permute-done((f16[1,1,2,64,512]{4,3,2,1,0:T(8,128)(2,1)S(1)}, f16[1,1,2,64,512]{4,3,2,1,0:T(8,128)(2,1)S(1)}, u32[]{:S(2)}, u32[]{:S(2)}) %collective-permute-start.17) | collective-permute-done | bytes 131104 | tf_op jit(solution)/shard_map/ppermute | solution.py:31
  66.2 2.8 %collective-permute-start.18 = (f16[1,1,1,64,512]{4,3,2,1,0:T(8,128)(2,1)S(1)}, f16[1,1,1,64,512]{4,3,2,1,0:T(8,128)(2,1)S(1)}, u32[]{:S(2)}, u32[]{:S(2)}) collective-permute-start(f16[1,1,1,64,512]{4,3,2,1,0:T(8,128)(2,1)S(1)} %slice_convert_fusion.6), channel_id=1, source_target_pairs={{0,8},{1,9},{2,10},{3,11},{4,12},{5,13},{6,14},{7,15},{8,0},{9,1},... | collective-permute-start | bytes 196616 | tf_op jit(solution)/shard_map/ppermute | solution.py:31
  69.9 1.1 %collective-permute-start.12 = (f16[1,1,1,64,512]{4,3,2,1,0:T(8,128)(2,1)S(1)}, f16[1,1,1,64,512]{4,3,2,1,0:T(8,128)(2,1)S(1)}, u32[]{:S(2)}, u32[]{:S(2)}) collective-permute-start(f16[1,1,1,64,512]{4,3,2,1,0:T(8,128)(2,1)S(1)} %slice_convert_fusion.7), channel_id=1, source_target_pairs={{0,2},{1,3},{2,0},{3,1},{4,6},{5,7},{6,4},{7,5},{8,10},{9,11},{10,... | collective-permute-start | bytes 196616 | tf_op jit(solution)/shard_map/ppermute | solution.py:31
  71.9 2.3 %collective-permute-done.12 = f16[1,1,1,64,512]{4,3,2,1,0:T(8,128)(2,1)S(1)} collective-permute-done((f16[1,1,1,64,512]{4,3,2,1,0:T(8,128)(2,1)S(1)}, f16[1,1,1,64,512]{4,3,2,1,0:T(8,128)(2,1)S(1)}, u32[]{:S(2)}, u32[]{:S(2)}) %collective-permute-start.12) | collective-permute-done | bytes 65568 | tf_op jit(solution)/shard_map/ppermute | solution.py:31
  75.2 1.6 %collective-permute-start.8 = (f16[1,1,2,64,1024]{4,3,2,1,0:T(8,128)(2,1)S(1)}, f16[1,1,2,64,1024]{4,3,2,1,0:T(8,128)(2,1)S(1)}, u32[]{:S(2)}, u32[]{:S(2)}) collective-permute-start(f16[1,1,2,64,1024]{4,3,2,1,0:T(8,128)(2,1)S(1)} %slice_convert_fusion.1), channel_id=1, source_target_pairs={{0,4},{1,5},{2,6},{3,7},{4,0},{5,1},{6,2},{7,3},{8,12},{9,13},{10,... | collective-permute-start | bytes 786440 | tf_op jit(solution)/shard_map/ppermute | solution.py:31
  76.8 5.5 %collective-permute-done.14 = f16[1,1,2,64,1024]{4,3,2,1,0:T(8,128)(2,1)S(1)} collective-permute-done((f16[1,1,2,64,1024]{4,3,2,1,0:T(8,128)(2,1)S(1)}, f16[1,1,2,64,1024]{4,3,2,1,0:T(8,128)(2,1)S(1)}, u32[]{:S(2)}, u32[]{:S(2)}) %collective-permute-start.14) | collective-permute-done | bytes 262176 | tf_op jit(solution)/shard_map/ppermute | solution.py:31
  82.4 2.6 %collective-permute-start.15 = (f16[1,1,1,64,1024]{4,3,2,1,0:T(8,128)(2,1)S(1)}, f16[1,1,1,64,1024]{4,3,2,1,0:T(8,128)(2,1)S(1)}, u32[]{:S(2)}, u32[]{:S(2)}) collective-permute-start(f16[1,1,1,64,1024]{4,3,2,1,0:T(8,128)(2,1)S(1)} %slice_convert_fusion.3), channel_id=1, source_target_pairs={{0,8},{1,9},{2,10},{3,11},{4,12},{5,13},{6,14},{7,15},{8,0},{9,1},... | collective-permute-start | bytes 393224 | tf_op jit(solution)/shard_map/ppermute | solution.py:31
  85.0 1.5 %collective-permute-done.8 = f16[1,1,2,64,1024]{4,3,2,1,0:T(8,128)(2,1)S(1)} collective-permute-done((f16[1,1,2,64,1024]{4,3,2,1,0:T(8,128)(2,1)S(1)}, f16[1,1,2,64,1024]{4,3,2,1,0:T(8,128)(2,1)S(1)}, u32[]{:S(2)}, u32[]{:S(2)}) %collective-permute-start.8) | collective-permute-done | bytes 262176 | tf_op jit(solution)/shard_map/ppermute | solution.py:31
  86.6 2.6 %collective-permute-start.9 = (f16[1,1,1,64,1024]{4,3,2,1,0:T(8,128)(2,1)S(1)}, f16[1,1,1,64,1024]{4,3,2,1,0:T(8,128)(2,1)S(1)}, u32[]{:S(2)}, u32[]{:S(2)}) collective-permute-start(f16[1,1,1,64,1024]{4,3,2,1,0:T(8,128)(2,1)S(1)} %slice_convert_fusion.5), channel_id=1, source_target_pairs={{0,8},{1,9},{2,10},{3,11},{4,12},{5,13},{6,14},{7,15},{8,0},{9,1},... | collective-permute-start | bytes 393224 | tf_op jit(solution)/shard_map/ppermute | solution.py:31
  89.2 4.7 %collective-permute-done.9 = f16[1,1,1,64,1024]{4,3,2,1,0:T(8,128)(2,1)S(1)} collective-permute-done((f16[1,1,1,64,1024]{4,3,2,1,0:T(8,128)(2,1)S(1)}, f16[1,1,1,64,1024]{4,3,2,1,0:T(8,128)(2,1)S(1)}, u32[]{:S(2)}, u32[]{:S(2)}) %collective-permute-start.9) | collective-permute-done | bytes 131104 | tf_op jit(solution)/shard_map/ppermute | solution.py:31
  (61 shorter events, 8.4 us)
Async XLA Ops:
  0.0 1.6 %copy-start = (bf16[1024,1024]{1,0:T(8,128)(2,1)S(1)}, bf16[1024,1024]{1,0:T(8,128)(2,1)}, u32[]{:S(2)}) copy-start(bf16[1024,1024]{1,0:T(8,128)(2,1)} %param.6) | copy-start | bytes 6291460
  0.0 38.2 %collective-permute-start.6 = (bf16[2,256,3072]{2,1,0:T(8,128)(2,1)}, bf16[2,256,3072]{2,1,0:T(8,128)(2,1)}, u32[]{:S(2)}, u32[]{:S(2)}) collective-permute-start(bf16[2,256,3072]{2,1,0:T(8,128)(2,1)} %own_x.7), channel_id=1, source_target_pairs={{0,1},{1,0},{2,3},{3,2},{4,5},{5,4},{6,7},{7,6},{8,9},{9,8},{10,11... | collective-permute-start | bytes 9437192 | tf_op jit(solution)/shard_map/ppermute | solution.py:31
  4.5 16.4 %collective-permute-start = (bf16[512,1024]{1,0:T(8,128)(2,1)S(1)}, bf16[512,1024]{1,0:T(8,128)(2,1)}, u32[]{:S(2)}, u32[]{:S(2)}) collective-permute-start(bf16[512,1024]{1,0:T(8,128)(2,1)S(1)} %fusion.7.own_ref), channel_id=1, source_target_pairs={{0,1},{1,0},{2,3},{3,2},{4,5},{5,4},{6,7},{7,6},{8,9},{9,8},{10,11... | collective-permute-start | bytes 3145736 | tf_op jit(solution)/shard_map/ppermute | solution.py:31
  9.1 6.6 %collective-permute-start.1 = (f32[8,512]{1,0:T(8,128)}, f32[8,512]{1,0:T(8,128)S(1)}, u32[]{:S(2)}, u32[]{:S(2)}) collective-permute-start(f32[8,512]{1,0:T(8,128)} %shard_map.47.mine_ref), channel_id=1, source_target_pairs={{0,16},{16,0},{1,17},{17,1},{2,18},{18,2},{3,19},{19,3},{4,20},{20... | collective-permute-start | bytes 49160 | tf_op jit(solution)/shard_map/ppermute | solution.py:31
  15.7 0.6 copy-start.3
  20.6 4.4 %copy-start.2 = (f32[8,896]{1,0:T(8,128)S(1)}, f32[8,896]{1,0:T(8,128)}, u32[]{:S(2)}) copy-start(f32[8,896]{1,0:T(8,128)} %shard_map.48.power_ref) | copy-start | bytes 86020
  20.6 15.0 %copy-start.1 = (f32[8,512]{1,0:T(8,128)S(1)}, f32[8,512]{1,0:T(8,128)}, u32[]{:S(2)}) copy-start(f32[8,512]{1,0:T(8,128)} %shard_map.47.mine_ref) | copy-start | bytes 49156
  20.6 15.0 %copy-start.4 = (f32[8,512]{1,0:T(8,128)S(1)}, f32[8,512]{1,0:T(8,128)}, u32[]{:S(2)}) copy-start(f32[8,512]{1,0:T(8,128)} %copy-done.3) | copy-start | bytes 49156
  20.6 4.4 %collective-permute-start.2 = (f32[8,896]{1,0:T(8,128)}, f32[8,896]{1,0:T(8,128)S(1)}, u32[]{:S(2)}, u32[]{:S(2)}) collective-permute-start(f32[8,896]{1,0:T(8,128)} %shard_map.48.power_ref), channel_id=1, source_target_pairs={{0,1},{1,0},{2,3},{3,2},{4,5},{5,4},{6,7},{7,6},{8,9},{9,8},{10,11... | collective-permute-start | bytes 86024 | tf_op jit(solution)/shard_map/ppermute | solution.py:31
  20.9 1.2 %copy-start.5 = (bf16[512,1024]{1,0:T(8,128)(2,1)S(1)}, bf16[512,1024]{1,0:T(8,128)(2,1)}, u32[]{:S(2)}) copy-start(bf16[512,1024]{1,0:T(8,128)(2,1)} %fusion.9.sel_ref) | copy-start | bytes 3145732
  25.0 4.0 %collective-permute-start.3 = (f32[8,1024]{1,0:T(8,128)S(1)}, f32[8,1024]{1,0:T(8,128)S(1)}, u32[]{:S(2)}, u32[]{:S(2)}) collective-permute-start(f32[8,1024]{1,0:T(8,128)S(1)} %shard_map.49.mine_ref), channel_id=1, source_target_pairs={{0,2},{1,3},{2,0},{3,1},{4,6},{5,7},{6,4},{7,5},{8,10},{9,11},{10,... | collective-permute-start | bytes 98312 | tf_op jit(solution)/shard_map/ppermute | solution.py:31
  29.0 4.0 %collective-permute-start.4 = (f32[8,1024]{1,0:T(8,128)S(1)}, f32[8,1024]{1,0:T(8,128)S(1)}, u32[]{:S(2)}, u32[]{:S(2)}) collective-permute-start(f32[8,1024]{1,0:T(8,128)S(1)} %shard_map.50.mine_ref), channel_id=1, source_target_pairs={{0,4},{1,5},{2,6},{3,7},{4,0},{5,1},{6,2},{7,3},{8,12},{9,13},{10,... | collective-permute-start | bytes 98312 | tf_op jit(solution)/shard_map/ppermute | solution.py:31
  33.0 4.8 %collective-permute-start.5 = (f32[8,1024]{1,0:T(8,128)S(1)}, f32[8,1024]{1,0:T(8,128)S(1)}, u32[]{:S(2)}, u32[]{:S(2)}) collective-permute-start(f32[8,1024]{1,0:T(8,128)S(1)} %shard_map.51.mine_ref), channel_id=1, source_target_pairs={{0,8},{1,9},{2,10},{3,11},{4,12},{5,13},{6,14},{7,15},{8,0},{9,1},... | collective-permute-start | bytes 98312 | tf_op jit(solution)/shard_map/ppermute | solution.py:31
  42.1 18.7 %collective-permute-start.16 = (f16[1,2,2,64,512]{4,3,2,1,0:T(8,128)(2,1)S(1)}, f16[1,2,2,64,512]{4,3,2,1,0:T(8,128)(2,1)S(1)}, u32[]{:S(2)}, u32[]{:S(2)}) collective-permute-start(f16[1,2,2,64,512]{4,3,2,1,0:T(8,128)(2,1)S(1)} %bitcast.29), channel_id=1, source_target_pairs={{0,2},{1,3},{2,0},{3,1},{4,6},{5,7},{6,4},{7,5},{8,10},{9,11},{10,... | collective-permute-start | bytes 786440 | tf_op jit(solution)/shard_map/ppermute | solution.py:31
  48.4 25.8 %collective-permute-start.13 = (f16[1,2,2,64,1024]{4,3,2,1,0:T(8,128)(2,1)S(1)}, f16[1,2,2,64,1024]{4,3,2,1,0:T(8,128)(2,1)S(1)}, u32[]{:S(2)}, u32[]{:S(2)}) collective-permute-start(f16[1,2,2,64,1024]{4,3,2,1,0:T(8,128)(2,1)S(1)} %bitcast.27), channel_id=1, source_target_pairs={{0,2},{1,3},{2,0},{3,1},{4,6},{5,7},{6,4},{7,5},{8,10},{9,11},{10,... | collective-permute-start | bytes 1572872 | tf_op jit(solution)/shard_map/ppermute | solution.py:31
  52.9 8.6 %collective-permute-start.10 = (f16[2,1,2,64,512]{4,3,2,1,0:T(8,128)(2,1)S(1)}, f16[2,1,2,64,512]{4,3,2,1,0:T(8,128)(2,1)S(1)}, u32[]{:S(2)}, u32[]{:S(2)}) collective-permute-start(f16[2,1,2,64,512]{4,3,2,1,0:T(8,128)(2,1)S(1)} %fusion.13), channel_id=1, source_target_pairs={{0,4},{1,5},{2,6},{3,7},{4,0},{5,1},{6,2},{7,3},{8,12},{9,13},{10,... | collective-permute-start | bytes 786440 | tf_op jit(solution)/shard_map/ppermute | solution.py:31
  59.3 15.7 %collective-permute-start.7 = (f16[1,2,2,64,1024]{4,3,2,1,0:T(8,128)(2,1)S(1)}, f16[1,2,2,64,1024]{4,3,2,1,0:T(8,128)(2,1)S(1)}, u32[]{:S(2)}, u32[]{:S(2)}) collective-permute-start(f16[1,2,2,64,1024]{4,3,2,1,0:T(8,128)(2,1)S(1)} %bitcast.28), channel_id=1, source_target_pairs={{0,2},{1,3},{2,0},{3,1},{4,6},{5,7},{6,4},{7,5},{8,10},{9,11},{10,... | collective-permute-start | bytes 1572872 | tf_op jit(solution)/shard_map/ppermute | solution.py:31
  61.0 5.2 %collective-permute-start.17 = (f16[1,1,2,64,512]{4,3,2,1,0:T(8,128)(2,1)S(1)}, f16[1,1,2,64,512]{4,3,2,1,0:T(8,128)(2,1)S(1)}, u32[]{:S(2)}, u32[]{:S(2)}) collective-permute-start(f16[1,1,2,64,512]{4,3,2,1,0:T(8,128)(2,1)S(1)} %slice_convert_fusion.2), channel_id=1, source_target_pairs={{0,4},{1,5},{2,6},{3,7},{4,0},{5,1},{6,2},{7,3},{8,12},{9,13},{10,... | collective-permute-start | bytes 393224 | tf_op jit(solution)/shard_map/ppermute | solution.py:31
  61.6 8.3 %collective-permute-start.11 = (f16[2,1,1,64,512]{4,3,2,1,0:T(8,128)(2,1)S(1)}, f16[2,1,1,64,512]{4,3,2,1,0:T(8,128)(2,1)S(1)}, u32[]{:S(2)}, u32[]{:S(2)}) collective-permute-start(f16[2,1,1,64,512]{4,3,2,1,0:T(8,128)(2,1)S(1)} %slice_convert_fusion.4), channel_id=1, source_target_pairs={{0,8},{1,9},{2,10},{3,11},{4,12},{5,13},{6,14},{7,15},{8,0},{9,1},... | collective-permute-start | bytes 393224 | tf_op jit(solution)/shard_map/ppermute | solution.py:31
  66.2 5.7 %collective-permute-start.18 = (f16[1,1,1,64,512]{4,3,2,1,0:T(8,128)(2,1)S(1)}, f16[1,1,1,64,512]{4,3,2,1,0:T(8,128)(2,1)S(1)}, u32[]{:S(2)}, u32[]{:S(2)}) collective-permute-start(f16[1,1,1,64,512]{4,3,2,1,0:T(8,128)(2,1)S(1)} %slice_convert_fusion.6), channel_id=1, source_target_pairs={{0,8},{1,9},{2,10},{3,11},{4,12},{5,13},{6,14},{7,15},{8,0},{9,1},... | collective-permute-start | bytes 196616 | tf_op jit(solution)/shard_map/ppermute | solution.py:31
  69.9 4.3 %collective-permute-start.12 = (f16[1,1,1,64,512]{4,3,2,1,0:T(8,128)(2,1)S(1)}, f16[1,1,1,64,512]{4,3,2,1,0:T(8,128)(2,1)S(1)}, u32[]{:S(2)}, u32[]{:S(2)}) collective-permute-start(f16[1,1,1,64,512]{4,3,2,1,0:T(8,128)(2,1)S(1)} %slice_convert_fusion.7), channel_id=1, source_target_pairs={{0,2},{1,3},{2,0},{3,1},{4,6},{5,7},{6,4},{7,5},{8,10},{9,11},{10,... | collective-permute-start | bytes 196616 | tf_op jit(solution)/shard_map/ppermute | solution.py:31
  74.4 7.8 %collective-permute-start.14 = (f16[1,1,2,64,1024]{4,3,2,1,0:T(8,128)(2,1)S(1)}, f16[1,1,2,64,1024]{4,3,2,1,0:T(8,128)(2,1)S(1)}, u32[]{:S(2)}, u32[]{:S(2)}) collective-permute-start(f16[1,1,2,64,1024]{4,3,2,1,0:T(8,128)(2,1)S(1)} %slice_convert_fusion), channel_id=1, source_target_pairs={{0,4},{1,5},{2,6},{3,7},{4,0},{5,1},{6,2},{7,3},{8,12},{9,13},{10,... | collective-permute-start | bytes 786440 | tf_op jit(solution)/shard_map/ppermute | solution.py:31
  75.2 11.3 %collective-permute-start.8 = (f16[1,1,2,64,1024]{4,3,2,1,0:T(8,128)(2,1)S(1)}, f16[1,1,2,64,1024]{4,3,2,1,0:T(8,128)(2,1)S(1)}, u32[]{:S(2)}, u32[]{:S(2)}) collective-permute-start(f16[1,1,2,64,1024]{4,3,2,1,0:T(8,128)(2,1)S(1)} %slice_convert_fusion.1), channel_id=1, source_target_pairs={{0,4},{1,5},{2,6},{3,7},{4,0},{5,1},{6,2},{7,3},{8,12},{9,13},{10,... | collective-permute-start | bytes 786440 | tf_op jit(solution)/shard_map/ppermute | solution.py:31
  82.4 6.8 %collective-permute-start.15 = (f16[1,1,1,64,1024]{4,3,2,1,0:T(8,128)(2,1)S(1)}, f16[1,1,1,64,1024]{4,3,2,1,0:T(8,128)(2,1)S(1)}, u32[]{:S(2)}, u32[]{:S(2)}) collective-permute-start(f16[1,1,1,64,1024]{4,3,2,1,0:T(8,128)(2,1)S(1)} %slice_convert_fusion.3), channel_id=1, source_target_pairs={{0,8},{1,9},{2,10},{3,11},{4,12},{5,13},{6,14},{7,15},{8,0},{9,1},... | collective-permute-start | bytes 393224 | tf_op jit(solution)/shard_map/ppermute | solution.py:31
  86.6 7.3 %collective-permute-start.9 = (f16[1,1,1,64,1024]{4,3,2,1,0:T(8,128)(2,1)S(1)}, f16[1,1,1,64,1024]{4,3,2,1,0:T(8,128)(2,1)S(1)}, u32[]{:S(2)}, u32[]{:S(2)}) collective-permute-start(f16[1,1,1,64,1024]{4,3,2,1,0:T(8,128)(2,1)S(1)} %slice_convert_fusion.5), channel_id=1, source_target_pairs={{0,8},{1,9},{2,10},{3,11},{4,12},{5,13},{6,14},{7,15},{8,0},{9,1},... | collective-permute-start | bytes 393224 | tf_op jit(solution)/shard_map/ppermute | solution.py:31
